TPU v7x, 512 devices: a whole 4x4x16 slice. The times are simulated.
512 devices in a mesh: dp: 8 (over y, core), expert: 64 (over x, z).
Axes of the slice: x: 4, y: 4, z: 16, core: 2. Of those that a mesh axis runs over, the one named last changes fastest.
Arguments:
- attn: bfloat16 [64, 256, 4096], P('expert', None, 'dp'), may hold values from -6 to 6
- resid: bfloat16 [64, 256, 2048], P('expert', 'dp'), may hold values from -6 to 6
- w_out: bfloat16 [4096, 2048], P('dp', 'expert'), may hold values from -0.09375 to 0.09375
- gain_post: float32 [2048], replicated, may hold values from 0.1 to 1.9
- route_ids: int32 [64, 256, 8], P('expert', 'dp'), may hold values from 0 to 63, all different within a row; in each aligned block of 32 rows (0 to 31, 32 to 63, ..., all dimensions but the last counted through in order) at most 8 rows name the same one
- route_logits: float32 [64, 256, 8], P('expert', 'dp'), may hold values from -2 to 260
- live_count: int32 [64, 8], P('expert', 'dp'), may hold values from 1 to 32, as said below
- w_gate_up: bfloat16 [64, 2048, 1536], P('expert', 'dp'), may hold values from -0.125 to 0.125
- w_down: bfloat16 [64, 768, 2048], P('expert', None, 'dp'), may hold values from -0.21875 to 0.21875
- gain_final: float32 [2048], replicated, may hold values from 0.1 to 1.9
Outputs:
- stream_out: bfloat16 [64, 256, 2048], P('expert', 'dp')
- normed_out: bfloat16 [64, 256, 2048], P('expert', 'dp')
Inputs may be any that keep to these rules, and one draw needn't show every extreme that they name: `route_ids`: each row names 8 different experts; among the rows of one device no expert is named more than 8 times. `live_count`: the devices whose dp index is a multiple of 3 hold prefill rows, all live; the others hold decode rows with a varying count.
All inputs are finite; a program needn't handle non-finite values.
Results may differ from a plain program's by a relative error of at most 0.018.
Values may be sent and summed in bfloat16 or wider, within the bound.
A program may use at most 64 MiB of HBM per device.

v0:
```python
import math

import jax
import jax.numpy as jnp
from jax import lax
from jax.sharding import PartitionSpec as P


def rms_scale(values, gain):
    return values * lax.rsqrt(jnp.mean(values * values, axis=-1, keepdims=True) + 1e-06) * gain


def swiglu_rows(rows_in, gate_up, down, hidden_units):
    both = jnp.dot(rows_in, gate_up, preferred_element_type=jnp.float32)
    inner = (jax.nn.silu(both[:, :hidden_units]) * both[:, hidden_units:]).astype(jnp.bfloat16)
    return jnp.dot(inner, down, preferred_element_type=jnp.float32).astype(jnp.bfloat16)


def body(
    attn,
    resid,
    w_out,
    gain_post,
    route_ids,
    route_logits,
    live_count,
    w_gate_up,
    w_down,
    gain_final,
):
    rows_here = resid.shape[1]
    model_width = resid.shape[2]
    top_count = route_ids.shape[2]
    dp_count = lax.axis_size("dp")
    expert_count = lax.axis_size("expert")
    hidden_units = w_down.shape[1]
    capacity = dp_count * max(1, 2 * rows_here * top_count // (expert_count * dp_count))
    slot_count = expert_count * capacity
    flat_attn = attn[0]
    partial_out = jnp.dot(
        flat_attn,
        lax.all_gather(w_out, "expert", axis=1, tiled=True),
        preferred_element_type=jnp.float32,
    )
    projected = lax.psum_scatter(
        partial_out.astype(jnp.bfloat16), "dp", scatter_dimension=0, tiled=True
    ).astype(jnp.float32)
    stream_in = (resid[0].astype(jnp.float32) + projected).astype(jnp.bfloat16)
    stream_float = stream_in.astype(jnp.float32)
    normed_in = rms_scale(stream_float, gain_post).astype(jnp.bfloat16)
    probs = jax.nn.softmax(route_logits[0], axis=-1).astype(jnp.bfloat16)
    alive = jnp.arange(rows_here, dtype=jnp.int32) < live_count[0, 0]
    expert_of = route_ids[0].reshape(-1)
    route_alive = jnp.repeat(alive, top_count)
    onehot = (
        (expert_of[:, None] == jnp.arange(expert_count, dtype=jnp.int32)[None, :])
        & route_alive[:, None]
    ).astype(jnp.int32)
    earlier = jnp.sum((jnp.cumsum(onehot, axis=0) - onehot) * onehot, axis=1)
    target = expert_of * capacity + earlier
    match = (target[:, None] == jnp.arange(slot_count, dtype=jnp.int32)[None, :]) & route_alive[
        :, None
    ]
    placed = match.reshape(rows_here, top_count, slot_count)
    gather_matrix = jnp.any(placed, axis=1).astype(jnp.bfloat16)
    send_rows = lax.dot_general(
        gather_matrix, normed_in, (((0,), (0,)), ((), ())), preferred_element_type=jnp.float32
    ).astype(jnp.bfloat16)
    send_flags = jnp.sum(gather_matrix.astype(jnp.float32), axis=0).astype(jnp.bfloat16)
    combine_matrix = jnp.sum(
        jnp.where(placed, probs.astype(jnp.float32)[:, :, None], jnp.float32(0.0)), axis=1
    ).astype(jnp.bfloat16)
    arrived_rows, arrived_flags = (
        lax.all_to_all(
            send_rows.reshape(expert_count, capacity, model_width),
            "expert",
            split_axis=0,
            concat_axis=0,
            tiled=True,
        ),
        lax.all_to_all(
            send_flags.reshape(expert_count, capacity),
            "expert",
            split_axis=0,
            concat_axis=0,
            tiled=True,
        ),
    )
    arrived = arrived_rows.reshape(slot_count, model_width)
    flags = arrived_flags.reshape(slot_count)
    gate_up_full, down_full = (
        lax.all_gather(w_gate_up, "dp", axis=1, tiled=True),
        lax.all_gather(w_down, "dp", axis=2, tiled=True),
    )
    live_slot = (flags > 0.5).astype(jnp.int32)
    order = jnp.argsort(1 - live_slot, stable=True)
    live_total = jnp.sum(live_slot)
    packed = arrived[order]
    block_len = math.gcd(slot_count, 128)
    block_total = (live_total + block_len - 1) // block_len

    def run_block(index, outputs):
        begin = index * block_len
        rows_in = lax.dynamic_slice_in_dim(packed, begin, block_len, 0)
        block_out = swiglu_rows(rows_in, gate_up_full[0], down_full[0], hidden_units)
        return lax.dynamic_update_slice_in_dim(outputs, block_out, begin, 0)

    packed_out = lax.fori_loop(
        0, block_total, run_block, jnp.zeros((slot_count, model_width), jnp.bfloat16)
    )
    position = (
        jnp.zeros((slot_count,), jnp.int32).at[order].set(jnp.arange(slot_count, dtype=jnp.int32))
    )
    results = packed_out[position]
    returned = lax.all_to_all(
        results.reshape(expert_count, capacity, model_width),
        "expert",
        split_axis=0,
        concat_axis=0,
        tiled=True,
    )
    returned = returned.reshape(slot_count, model_width)
    mixture = jnp.dot(combine_matrix, returned, preferred_element_type=jnp.float32)
    stream_out = (stream_float + mixture).astype(jnp.bfloat16)
    normed_out = rms_scale(stream_out.astype(jnp.float32), gain_final).astype(jnp.bfloat16)
    return (stream_out[None], normed_out[None])


def solution(mesh):
    placed = (
        P("expert", None, "dp"),
        P("expert", "dp", None),
        P("dp", "expert"),
        P(),
        P("expert", "dp", None),
        P("expert", "dp", None),
        P("expert", "dp"),
        P("expert", "dp", None),
        P("expert", None, "dp"),
        P(),
    )
    return jax.shard_map(
        body,
        mesh=mesh,
        in_specs=placed,
        out_specs=(P("expert", "dp", None), P("expert", "dp", None)),
        check_vma=False,
    )
```

profile of v0, /device:TPU:62, one launch (start us, length us, event | category | flops | bytes accessed | tf_op | source)
XLA Modules:
  0.0 446.4 jit_solution(4035155335407149647)
XLA Ops:
  7.2 0.7 all-gather.4.cloned.1.call-update
  8.0 146.4 %all-gather.4.cloned.1.call-done = bf16[512,2048]{0,1:T(8,128)(2,1)} async-done(((bf16[512,32]{0,1:T(8,128)(2,1)}), bf16[512,2048]{0,1:T(8,128)(2,1)}) %all-gather.4.cloned.1.call-update) | async-done | bytes 2097168 | tf_op jit(solution)/shard_map/all_gather | solution.py:42
  154.4 3.3 convolution_convert_fusion.1
  157.7 0.7 all-gather.8.cloned.1.call-update
  160.1 0.6 reduce-window.6
  161.7 0.7 all_to_all.16
  162.4 11.8 %all-to-all-start = ((bf16[64,1,8]{2,1,0:T(2,128)(2,1)}), bf16[64,1,8]{2,1,0:T(2,128)(2,1)S(1)}, u32[]{:S(2)}, u32[]{:S(2)}) async-start(bf16[64,1,8]{2,1,0:T(2,128)(2,1)} %all_to_all.16), calls=%async_computation.1 | async-start | bytes 65536 | tf_op jit(solution)/shard_map/all_to_all | solution.py:81
  174.2 17.8 %reduce-scatter.2.cloned.1.call-done = bf16[32,2048]{1,0:T(8,128)(2,1)} async-done(((bf16[256,2048]{1,0:T(8,128)(2,1)}), bf16[32,2048]{1,0:T(8,128)(2,1)}) %reduce-scatter.2.cloned.1.call-update) | async-done | bytes 131088 | tf_op jit(solution)/shard_map/reduce_scatter | solution.py:45
  192.0 1.1 fusion.24
  193.1 3.0 fusion.16
  196.1 15.5 %all-to-all-start.1 = ((bf16[64,8,2048]{2,1,0:T(8,128)(2,1)}), bf16[64,8,2048]{2,1,0:T(8,128)(2,1)S(1)}, u32[]{:S(2)}, u32[]{:S(2)}) async-start(bf16[64,8,2048]{2,1,0:T(8,128)(2,1)} %fusion.16), calls=%async_computation.2 | async-start | bytes 4194304 | tf_op jit(solution)/shard_map/all_to_all | solution.py:74
  211.6 0.8 subtract_reduce_fusion
  213.1 3.8 sort.17
  216.9 2.4 scatter_custom_fusion
  219.4 91.3 %all-to-all-done.1 = bf16[64,8,2048]{2,1,0:T(8,128)(2,1)S(1)} async-done(((bf16[64,8,2048]{2,1,0:T(8,128)(2,1)}), bf16[64,8,2048]{2,1,0:T(8,128)(2,1)S(1)}, u32[]{:S(2)}, u32[]{:S(2)}) %all-to-all-start.1) | async-done | bytes 2097184 | tf_op jit(solution)/shard_map/all_to_all | solution.py:74
  310.6 3.3 gather_fusion
  314.2 9.5 %while.10 = (s32[]{:T(128)}, bf16[512,2048]{1,0:T(8,128)(2,1)S(1)}, s32[]{:T(128)}, bf16[512,2048]{1,0:T(8,128)(2,1)}, bf16[1,2048,1536]{2,1,0:T(8,128)(2,1)}, /...) while((s32[]{:T(128)}, bf16[512,2048]{1,0:T(8,128)(2,1)S(1)}, ...), condition=%wide.region_13.14_spmd, body=%wide.region_12.13_spmd.sunk | while | flops 1208811520 | bytes 24641720 | solution.py:108
  314.2 4.1 fusion.60
  319.0 4.1 fusion.60
  323.1 0.6 fusion.61
  323.7 3.3 gather_fusion.1
  327.1 17.5 %all-to-all-start.2 = ((bf16[64,8,2048]{2,1,0:T(8,128)(2,1)}), bf16[64,8,2048]{2,1,0:T(8,128)(2,1)S(1)}, u32[]{:S(2)}, u32[]{:S(2)}) async-start(bf16[64,8,2048]{2,1,0:T(8,128)(2,1)} %bitcast.77), calls=%async_computation.3 | async-start | bytes 4194304 | tf_op jit(solution)/shard_map/all_to_all | solution.py:115
  345.0 93.5 %all-to-all-done.2 = bf16[64,8,2048]{2,1,0:T(8,128)(2,1)S(1)} async-done(((bf16[64,8,2048]{2,1,0:T(8,128)(2,1)}), bf16[64,8,2048]{2,1,0:T(8,128)(2,1)S(1)}, u32[]{:S(2)}, u32[]{:S(2)}) %all-to-all-start.2) | async-done | bytes 2097184 | tf_op jit(solution)/shard_map/all_to_all | solution.py:115
  439.1 0.8 fusion.30
  (64 shorter events, 4.1 us)
Async XLA Ops:
  7.2 147.2 %copy-start = (bf16[1,256,512]{2,1,0:T(8,128)(2,1)S(1)}, bf16[1,256,512]{2,1,0:T(8,128)(2,1)}, u32[]{:S(2)}) copy-start(bf16[1,256,512]{2,1,0:T(8,128)(2,1)} %param.12) | copy-start | bytes 786436
  7.2 147.2 %all-gather.4.cloned.1.call-start = ((), (), s32[]{:S(2)}) async-start(), calls=%async_computation.4 | async-start | bytes 2129920 | tf_op jit(solution)/shard_map/all_gather | solution.py:42
  7.9 151.1 %copy-start.7 = (s32[1,32,8]{1,2,0:T(8,128)S(1)}, s32[1,32,8]{1,2,0:T(8,128)}, u32[]{:S(2)}) copy-start(s32[1,32,8]{1,2,0:T(8,128)} %param.16) | copy-start | bytes 3076
  7.9 184.1 %reduce-scatter.2.cloned.1.call-start = ((), (), s32[]{:S(2)}) async-start(), calls=%async_computation.5 | async-start | bytes 1179648 | tf_op jit(solution)/shard_map/reduce_scatter | solution.py:45
  157.7 34.3 %copy-start.1 = (bf16[1,32,2048]{2,1,0:T(8,128)(2,1)S(1)}, bf16[1,32,2048]{2,1,0:T(8,128)(2,1)}, u32[]{:S(2)}) copy-start(bf16[1,32,2048]{2,1,0:T(8,128)(2,1)} %param.13) | copy-start | bytes 393220
  157.7 35.4 %copy-start.5 = (f32[2048]{0:T(1024)S(1)}, f32[2048]{0:T(1024)}, u32[]{:S(2)}) copy-start(f32[2048]{0:T(1024)} %param.15) | copy-start | bytes 24580
  157.7 156.2 %all-gather.8.cloned.1.call-start = ((), (), s32[]{:S(2)}) async-start(), calls=%async_computation.7 | async-start | bytes 3538944 | tf_op jit(solution)/shard_map/all_gather | solution.py:93
  158.4 155.5 %all-gather.6.cloned.1.call-start = ((), (), s32[]{:S(2)}) async-start(), calls=%async_computation.6 | async-start | bytes 7077888 | tf_op jit(solution)/shard_map/all_gather | solution.py:92
  162.4 33.7 %all-to-all-start = ((bf16[64,1,8]{2,1,0:T(2,128)(2,1)}), bf16[64,1,8]{2,1,0:T(2,128)(2,1)S(1)}, u32[]{:S(2)}, u32[]{:S(2)}) async-start(bf16[64,1,8]{2,1,0:T(2,128)(2,1)} %all_to_all.16), calls=%async_computation.1 | async-start | bytes 65536 | tf_op jit(solution)/shard_map/all_to_all | solution.py:81
  196.1 114.6 %all-to-all-start.1 = ((bf16[64,8,2048]{2,1,0:T(8,128)(2,1)}), bf16[64,8,2048]{2,1,0:T(8,128)(2,1)S(1)}, u32[]{:S(2)}, u32[]{:S(2)}) async-start(bf16[64,8,2048]{2,1,0:T(8,128)(2,1)} %fusion.16), calls=%async_computation.2 | async-start | bytes 4194304 | tf_op jit(solution)/shard_map/all_to_all | solution.py:74
  314.2 4.1 copy-start.8
  319.0 4.1 copy-start.8
  327.1 17.5 %copy-start.4 = (f32[1,32,8]{1,2,0:T(8,128)S(1)}, f32[1,32,8]{1,2,0:T(8,128)}, u32[]{:S(2)}) copy-start(f32[1,32,8]{1,2,0:T(8,128)} %param.17) | copy-start | bytes 3076
  327.1 111.4 %copy-start.2 = (bf16[32,2048]{1,0:T(8,128)(2,1)S(1)}, bf16[32,2048]{1,0:T(8,128)(2,1)}, u32[]{:S(2)}) copy-start(bf16[32,2048]{1,0:T(8,128)(2,1)} %reduce-scatter.2.cloned.1.call-done) | copy-start | bytes 393220
  327.1 111.4 %all-to-all-start.2 = ((bf16[64,8,2048]{2,1,0:T(8,128)(2,1)}), bf16[64,8,2048]{2,1,0:T(8,128)(2,1)S(1)}, u32[]{:S(2)}, u32[]{:S(2)}) async-start(bf16[64,8,2048]{2,1,0:T(8,128)(2,1)} %bitcast.77), calls=%async_computation.3 | async-start | bytes 4194304 | tf_op jit(solution)/shard_map/all_to_all | solution.py:115
  344.6 94.5 %copy-start.6 = (f32[2048]{0:T(1024)S(1)}, f32[2048]{0:T(1024)}, u32[]{:S(2)}) copy-start(f32[2048]{0:T(1024)} %param.21) | copy-start | bytes 24580
  439.1 0.8 copy-start.3
Sparse Core Ops, SparseCore 0:
  11.0 143.3 all-gather.3
  157.8 34.1 reduce-scatter.1
  194.1 40.4 all-gather.7
  236.6 49.6 all-gather.5
where the time goes:
time: 446 us
  waiting for transfers between devices  351 us (79%)
  starting transfers between devices  45 us (10%)
  matrix products  16.3 us (4%)
  between operations  15.3 us (3%)
  local copies, waits for them, and re-layouts  11.1 us (2%)
  other arithmetic  7.79 us (2%)
    all_gather x1, waiting for transfers between devices, body(): lax.all_gather(w_out, 'expert', axis=1, tiled=True)  146 us
    all_to_all x1, waiting for transfers between devices, body(): lax.all_to_all(results.reshape(expert_count, capacity, model_width), 'exp...  93.5 us
    all_to_all x1, waiting for transfers between devices, body(): lax.all_to_all(send_rows.reshape(expert_count, capacity, model_width), 'e...  91.3 us
    reduce_scatter x1, waiting for transfers between devices, body(): lax.psum_scatter(partial_out.astype(jnp.bfloat16), 'dp', scatter_dimensio...  17.8 us
    all_to_all x1, starting transfers between devices, body(): lax.all_to_all(results.reshape(expert_count, capacity, model_width), 'exp...  17.5 us
    all_to_all x1, starting transfers between devices, body(): lax.all_to_all(send_rows.reshape(expert_count, capacity, model_width), 'e...  15.5 us
    all_to_all x1, starting transfers between devices, body(): lax.all_to_all(send_flags.reshape(expert_count, capacity), 'expert', spli...  11.8 us
  transfers between devices with their start and end apart: 7, of which 4 were waited for; matrix products, arithmetic and copies ran while one was open for 4% of the time, Pallas kernels for 0%

commit v1 on v0

--- a/solution.py
+++ b/solution.py
@@ -3,7 +3,12 @@
 import jax
 import jax.numpy as jnp
 from jax import lax
+from jax.experimental import pallas as pl
+from jax.experimental.pallas import tpu as pltpu
 from jax.sharding import PartitionSpec as P
+
+NX, NZ, NY = 4, 16, 4
+MESH = pl.DeviceIdType.MESH
 
 
 def rms_scale(values, gain):
@@ -14,6 +19,202 @@
     both = jnp.dot(rows_in, gate_up, preferred_element_type=jnp.float32)
     inner = (jax.nn.silu(both[:, :hidden_units]) * both[:, hidden_units:]).astype(jnp.bfloat16)
     return jnp.dot(inner, down, preferred_element_type=jnp.float32).astype(jnp.bfloat16)
+
+
+def places():
+    dp = lax.axis_index("dp")
+    expert = lax.axis_index("expert")
+    return dp, expert // NZ, expert % NZ
+
+
+def greet(dp, x, z):
+    peers = [(dp, x * NZ + (z + 1) % NZ), (dp, x * NZ + (z + NZ - 1) % NZ)]
+    peers += [(dp, (x + step) % NX * NZ + z) for step in range(1, NX)]
+    peers += [((dp + step) % 8, x * NZ + z) for step in range(1, 8)]
+    barrier = pltpu.get_barrier_semaphore()
+    for peer in peers:
+        pl.semaphore_signal(barrier, inc=1, device_id=peer, device_id_type=MESH)
+    pl.semaphore_wait(barrier, len(peers))
+
+
+def remote(src, dst, send_sem, recv_sem, peer):
+    return pltpu.make_async_remote_copy(
+        src_ref=src,
+        dst_ref=dst,
+        send_sem=send_sem,
+        recv_sem=recv_sem,
+        device_id=peer,
+        device_id_type=MESH,
+    )
+
+
+def project_kernel(
+    attn_ref,
+    resid_ref,
+    w_ref,
+    gain_ref,
+    stream_ref,
+    normed_ref,
+    wbuf,
+    pbuf,
+    rbuf,
+    wz_send,
+    wz_recv,
+    wx_send,
+    wx_recv,
+    rs_send,
+    rs_recv,
+):
+    dp, x, z = places()
+    up, below = (dp, x * NZ + (z + 1) % NZ), (dp, x * NZ + (z + NZ - 1) % NZ)
+    right, left = (dp, (x + 1) % NX * NZ + z), (dp, (x + NX - 1) % NX * NZ + z)
+    greet(dp, x, z)
+    wbuf[x * NZ + z] = w_ref[...]
+
+    def block(column, side, h):
+        return wbuf.at[(x + column) % NX * NZ + (z + (h if side == 0 else NZ - h)) % NZ]
+
+    def z_copy(side, h):
+        ref = block(0, side if h else 0, h)
+        at = side * 8 + h
+        return remote(ref, ref, wz_send.at[at], wz_recv.at[at], below if side == 0 else up)
+
+    def z_arrival(side, h):
+        ref = block(0, side, h)
+        at = side * 8 + h - 1
+        return remote(ref, ref, wz_send.at[at], wz_recv.at[at], below if side == 0 else up)
+
+    def place(side, h):
+        return h if side == 0 else 7 + h
+
+    def x_copy(way, side, h):
+        at = way * 16 + place(side, h)
+        if way == 2:
+            ref = block(1, side, h) if side == 0 else block(3, side, h)
+            peer = left if side == 0 else right
+        else:
+            ref = block(0, side, h)
+            peer = right if way == 0 else left
+        return remote(ref, ref, wx_send.at[at], wx_recv.at[at], peer)
+
+    def x_arrival(way, side, h):
+        at = way * 16 + place(side, h)
+        ref = block((3, 1, 2)[way], side, h)
+        return remote(ref, ref, wx_send.at[at], wx_recv.at[at], right)
+
+    def steps(h):
+        return [(side, h) for side in (0, 1) if (side == 0 and h <= 7) or (side == 1 and h >= 1)]
+
+    for h in range(9):
+        if h == 0:
+            z_copy(0, 0).start()
+            z_copy(1, 0).start()
+        for side, at in steps(h):
+            if at:
+                z_arrival(side, at).wait_recv()
+                if at < (7 if side == 0 else 8):
+                    z_copy(side, at).start()
+            x_copy(0, side, at).start()
+            x_copy(1, side, at).start()
+        if h >= 2:
+            for side, at in steps(h - 2):
+                x_arrival(1 if side == 0 else 0, side, at).wait_recv()
+                x_copy(2, side, at).start()
+    for h in (7, 8):
+        for side, at in steps(h):
+            x_arrival(1 if side == 0 else 0, side, at).wait_recv()
+            x_copy(2, side, at).start()
+
+    every = [(side, h) for h in range(9) for side, _ in steps(h)]
+
+    def rs_copy(step, order, column):
+        target = (dp + step) % 8
+        at = (step - 1) * 4 + order
+        return remote(
+            pbuf.at[column, target],
+            rbuf.at[dp, column],
+            rs_send.at[at],
+            rs_recv.at[at],
+            (target, x * NZ + z),
+        )
+
+    for order in range(4):
+        column = (x + (0, 3, 1, 2)[order]) % NX
+        if order:
+            way = order - 1
+            for side, h in every:
+                if not (way == 0 and side == 1) and not (way == 1 and side == 0):
+                    x_arrival(way, side, h).wait_recv()
+        part = wbuf[pl.ds(column * NZ, NZ)].reshape(512, 512)
+        got = lax.dot_general(
+            attn_ref[...], part, (((1,), (1,)), ((), ())), preferred_element_type=jnp.float32
+        )
+        pbuf[column] = got.astype(jnp.bfloat16).reshape(8, 32, 512)
+        for step in range(1, 8):
+            rs_copy(step, order, column).start()
+
+    for order in range(4):
+        column = (x + (0, 3, 1, 2)[order]) % NX
+        for step in range(1, 8):
+            source = (dp + 8 - step) % 8
+            at = (step - 1) * 4 + order
+            remote(
+                pbuf.at[column, source],
+                rbuf.at[source, column],
+                rs_send.at[at],
+                rs_recv.at[at],
+                (source, x * NZ + z),
+            ).wait_recv()
+        rbuf[dp, column] = pbuf[column, dp]
+
+    square = jnp.zeros((32, 1), jnp.float32)
+    for g in range(4):
+        total = resid_ref[:, g * 512 : (g + 1) * 512].astype(jnp.float32)
+        proj = rbuf[0, g].astype(jnp.float32)
+        for source in range(1, 8):
+            proj += rbuf[source, g].astype(jnp.float32)
+        held = (total + proj).astype(jnp.bfloat16)
+        stream_ref[:, g * 512 : (g + 1) * 512] = held
+        wide = held.astype(jnp.float32)
+        square += jnp.sum(wide * wide, axis=-1, keepdims=True)
+    scale = lax.rsqrt(square / 2048.0 + 1e-06)
+    normed_ref[...] = (stream_ref[...].astype(jnp.float32) * scale * gain_ref[...]).astype(jnp.bfloat16)
+
+    z_copy(0, 0).wait_send()
+    z_copy(1, 0).wait_send()
+    for side, h in every:
+        if h and h < (7 if side == 0 else 8):
+            z_copy(side, h).wait_send()
+        for way in range(3):
+            x_copy(way, side, h).wait_send()
+    for order in range(4):
+        column = (x + (0, 3, 1, 2)[order]) % NX
+        for step in range(1, 8):
+            rs_copy(step, order, column).wait_send()
+
+
+def project(attn, resid, w_rows, gain):
+    vmem = pl.BlockSpec(memory_space=pltpu.VMEM)
+    return pl.pallas_call(
+        project_kernel,
+        out_shape=[jax.ShapeDtypeStruct((32, 2048), jnp.bfloat16)] * 2,
+        in_specs=[vmem] * 4,
+        out_specs=[vmem] * 2,
+        scratch_shapes=[
+            pltpu.VMEM((64, 32, 512), jnp.bfloat16),
+            pltpu.VMEM((4, 8, 32, 512), jnp.bfloat16),
+            pltpu.VMEM((8, 4, 32, 512), jnp.bfloat16),
+            pltpu.SemaphoreType.DMA((16,)),
+            pltpu.SemaphoreType.DMA((16,)),
+            pltpu.SemaphoreType.DMA((48,)),
+            pltpu.SemaphoreType.DMA((48,)),
+            pltpu.SemaphoreType.DMA((28,)),
+            pltpu.SemaphoreType.DMA((28,)),
+        ],
+        compiler_params=pltpu.CompilerParams(
+            collective_id=0, has_side_effects=True, vmem_limit_bytes=32 << 20
+        ),
+    )(attn, resid, w_rows, gain)
 
 
 def body(
@@ -36,18 +237,8 @@
     hidden_units = w_down.shape[1]
     capacity = dp_count * max(1, 2 * rows_here * top_count // (expert_count * dp_count))
     slot_count = expert_count * capacity
-    flat_attn = attn[0]
-    partial_out = jnp.dot(
-        flat_attn,
-        lax.all_gather(w_out, "expert", axis=1, tiled=True),
-        preferred_element_type=jnp.float32,
-    )
-    projected = lax.psum_scatter(
-        partial_out.astype(jnp.bfloat16), "dp", scatter_dimension=0, tiled=True
-    ).astype(jnp.float32)
-    stream_in = (resid[0].astype(jnp.float32) + projected).astype(jnp.bfloat16)
+    stream_in, normed_in = project(attn[0], resid[0], w_out.T, gain_post[None])
     stream_float = stream_in.astype(jnp.float32)
-    normed_in = rms_scale(stream_float, gain_post).astype(jnp.bfloat16)
     probs = jax.nn.softmax(route_logits[0], axis=-1).astype(jnp.bfloat16)
     alive = jnp.arange(rows_here, dtype=jnp.int32) < live_count[0, 0]
     expert_of = route_ids[0].reshape(-1)

time: 446 us -> 331 us (0.74)
  the two profiles are of different devices: /device:TPU:62 before, /device:TPU:16 now
where the time goes in v1:
time: 331 us; the launch traced here: 330 us
  waiting for transfers between devices  188 us (57%)
  Pallas kernels  56.3 us (17%)
  starting transfers between devices  41.3 us (12%)
  between operations  15.6 us (5%)
  local copies, waits for them, and re-layouts  15.1 us (5%)
  matrix products  7.34 us (2%)
  other arithmetic  6.73 us (2%)
    all_to_all x1, waiting for transfers between devices, body(): lax.all_to_all(results.reshape(expert_count, capacity, model_width), 'exp...  95.4 us
    all_to_all x1, waiting for transfers between devices, body(): lax.all_to_all(send_rows.reshape(expert_count, capacity, model_width), 'e...  90.9 us
    pallas_call x1, Pallas kernels, project(): pl.pallas_call(project_kernel, out_shape=[jax.ShapeDtypeStruct((32, 2048)...  56.3 us
    all_to_all x1, starting transfers between devices, body(): lax.all_to_all(send_flags.reshape(expert_count, capacity), 'expert', spli...  18.6 us
    all_to_all x1, starting transfers between devices, body(): lax.all_to_all(results.reshape(expert_count, capacity, model_width), 'exp...  17.9 us
  transfers between devices with their start and end apart: 5, of which 2 were waited for; matrix products, arithmetic and copies ran while one was open for 5% of the time, Pallas kernels for 17%

profile of v1, /device:TPU:16, one launch (start us, length us, event | category | flops | bytes accessed | tf_op | source)
XLA Modules:
  0.0 330.1 jit_solution(15348200249108209400)
XLA Ops:
  7.2 0.7 all-gather.5.cloned.1.call-update
  7.9 0.7 all-gather.3.cloned.1.call-update
  8.6 0.8 copy.25
  12.0 0.7 all_to_all.16
  12.7 18.6 %all-to-all-start = ((bf16[64,1,8]{2,1,0:T(2,128)(2,1)}), bf16[64,1,8]{2,1,0:T(2,128)(2,1)S(1)}, u32[]{:S(2)}, u32[]{:S(2)}) async-start(bf16[64,1,8]{2,1,0:T(2,128)(2,1)} %all_to_all.16), calls=%async_computation | async-start | bytes 65536 | tf_op jit(solution)/shard_map/all_to_all | solution.py:272
  31.3 1.0 copy-done
  32.3 0.9 copy-done.1
  33.2 0.8 copy-done.2
  34.0 0.7 copy-done.3
  34.7 56.3 %shard_map.113 = (bf16[32,2048]{1,0:T(8,128)(2,1)S(1)}, bf16[32,2048]{1,0:T(8,128)(2,1)S(1)}) custom-call(bf16[256,512]{1,0:T(8,128)(2,1)S(1)} %bitcast.67, bf16[32,2048]{1,0:T(8,128)(2,1)S(1)} %bitcast.68, bf16[32,512]{1,0:T(8,128)(2,1)S(1)} %bitcast.69, f32[1,2048]{1,0:T(1,128)S(1)} %bitcast.70), custom_call_target="tpu_custom_call" | custom-call | tf_op jit(solution)/shard_map/pallas_call | solution.py:198
  90.9 2.1 fusion.16
  93.0 4.7 %all-to-all-start.1 = ((bf16[64,8,2048]{2,1,0:T(8,128)(2,1)}), bf16[64,8,2048]{2,1,0:T(8,128)(2,1)S(1)}, u32[]{:S(2)}, u32[]{:S(2)}) async-start(bf16[64,8,2048]{2,1,0:T(8,128)(2,1)} %fusion.16), calls=%async_computation.1 | async-start | bytes 4194304 | tf_op jit(solution)/shard_map/all_to_all | solution.py:265
  97.7 0.8 subtract_reduce_fusion
  99.2 3.8 %sort.17 = (s32[512]{0:T(512)}, s32[512]{0:T(512)S(1)}) sort(s32[512]{0:T(512)S(1)} %sub.38, s32[512]{0:T(512)S(1)} %iota.44), dimensions={0}, to_apply=%region_9.10 | sort | flops 4608 | bytes 8192 | tf_op jit(solution)/shard_map/jit(argsort)/sort | solution.py:287
  103.0 2.4 scatter_custom_fusion
  105.5 90.9 %all-to-all-done.1 = bf16[64,8,2048]{2,1,0:T(8,128)(2,1)S(1)} async-done(((bf16[64,8,2048]{2,1,0:T(8,128)(2,1)}), bf16[64,8,2048]{2,1,0:T(8,128)(2,1)S(1)}, u32[]{:S(2)}, u32[]{:S(2)}) %all-to-all-start.1) | async-done | bytes 2097184 | tf_op jit(solution)/shard_map/all_to_all | solution.py:265
  196.4 3.3 gather_fusion
  200.0 4.8 %while.10 = (s32[]{:T(128)}, bf16[512,2048]{1,0:T(8,128)(2,1)S(1)}, s32[]{:T(128)}, bf16[512,2048]{1,0:T(8,128)(2,1)}, bf16[1,2048,1536]{2,1,0:T(8,128)(2,1)}, /...) while((s32[]{:T(128)}, bf16[512,2048]{1,0:T(8,128)(2,1)S(1)}, ...), condition=%wide.region_11.12_spmd, body=%wide.region_10.11_spmd.sunk | while | flops 1208811520 | bytes 24641720 | solution.py:299
  200.0 4.1 %fusion.51 = f32[128,1536]{1,0:T(8,128)S(1)} fusion(bf16[1,2048,1536]{2,1,0:T(8,128)(2,1)} %get-tuple-element.120, bf16[512,2048]{1,0:T(8,128)(2,1)} %get-tuple-element.119, s32[]{:T(128)S(6)} %select_n.28), kind=kOutput, calls=%fused_computation.3.clone.1 | convolution fusion | flops 805306368 | bytes 7602180 | tf_op jit(solution)/shard_map/while/body/dot_general | solution.py:19
  204.1 0.6 fusion.52
  204.8 3.3 %gather_fusion.1 = bf16[512,2048]{1,0:T(8,128)(2,1)} fusion(bf16[512,2048]{1,0:T(8,128)(2,1)S(1)} %get-tuple-element.41, s32[1024]{0:T(1024)S(1)} %pad_clamp_fusion), kind=kCustom, calls=%fused_computation.1 | custom fusion | bytes 4196352 | tf_op jit(solution)/shard_map/gather | solution.py:305
  208.1 17.9 %all-to-all-start.2 = ((bf16[64,8,2048]{2,1,0:T(8,128)(2,1)}), bf16[64,8,2048]{2,1,0:T(8,128)(2,1)S(1)}, u32[]{:S(2)}, u32[]{:S(2)}) async-start(bf16[64,8,2048]{2,1,0:T(8,128)(2,1)} %bitcast.72), calls=%async_computation.2 | async-start | bytes 4194304 | tf_op jit(solution)/shard_map/all_to_all | solution.py:306
  226.5 95.4 %all-to-all-done.2 = bf16[64,8,2048]{2,1,0:T(8,128)(2,1)S(1)} async-done(((bf16[64,8,2048]{2,1,0:T(8,128)(2,1)}), bf16[64,8,2048]{2,1,0:T(8,128)(2,1)S(1)}, u32[]{:S(2)}, u32[]{:S(2)}) %all-to-all-start.2) | async-done | bytes 2097184 | tf_op jit(solution)/shard_map/all_to_all | solution.py:306
  322.5 0.8 fusion.24
  (50 shorter events, 3.4 us)
Async XLA Ops:
  7.2 192.6 %all-gather.5.cloned.1.call-start = ((), (), s32[]{:S(2)}) async-start(), calls=%async_computation.4 | async-start | bytes 3538944 | tf_op jit(solution)/shard_map/all_gather | solution.py:284
  7.9 191.8 %all-gather.3.cloned.1.call-start = ((), (), s32[]{:S(2)}) async-start(), calls=%async_computation.3 | async-start | bytes 7077888 | tf_op jit(solution)/shard_map/all_gather | solution.py:283
  12.7 80.3 %all-to-all-start = ((bf16[64,1,8]{2,1,0:T(2,128)(2,1)}), bf16[64,1,8]{2,1,0:T(2,128)(2,1)S(1)}, u32[]{:S(2)}, u32[]{:S(2)}) async-start(bf16[64,1,8]{2,1,0:T(2,128)(2,1)} %all_to_all.16), calls=%async_computation | async-start | bytes 65536 | tf_op jit(solution)/shard_map/all_to_all | solution.py:272
  31.3 1.0 copy-start
  32.3 0.9 copy-start.1
  33.2 0.8 copy-start.2
  34.0 0.7 copy-start.3
  93.0 103.4 %all-to-all-start.1 = ((bf16[64,8,2048]{2,1,0:T(8,128)(2,1)}), bf16[64,8,2048]{2,1,0:T(8,128)(2,1)S(1)}, u32[]{:S(2)}, u32[]{:S(2)}) async-start(bf16[64,8,2048]{2,1,0:T(8,128)(2,1)} %fusion.16), calls=%async_computation.1 | async-start | bytes 4194304 | tf_op jit(solution)/shard_map/all_to_all | solution.py:265
  200.0 4.1 %copy-start.7 = (bf16[1,768,2048]{2,1,0:T(8,128)(2,1)S(1)}, bf16[1,768,2048]{2,1,0:T(8,128)(2,1)}, u32[]{:S(2)}) copy-start(bf16[1,768,2048]{2,1,0:T(8,128)(2,1)} %get-tuple-element.121) | copy-start | bytes 9437188 | tf_op jit(solution)/shard_map/while
  208.1 17.9 %copy-start.5 = (f32[1,32,8]{1,2,0:T(8,128)S(1)}, f32[1,32,8]{1,2,0:T(8,128)}, u32[]{:S(2)}) copy-start(f32[1,32,8]{1,2,0:T(8,128)} %param.17) | copy-start | bytes 3076
  208.1 113.8 %all-to-all-start.2 = ((bf16[64,8,2048]{2,1,0:T(8,128)(2,1)}), bf16[64,8,2048]{2,1,0:T(8,128)(2,1)S(1)}, u32[]{:S(2)}, u32[]{:S(2)}) async-start(bf16[64,8,2048]{2,1,0:T(8,128)(2,1)} %bitcast.72), calls=%async_computation.2 | async-start | bytes 4194304 | tf_op jit(solution)/shard_map/all_to_all | solution.py:306
  226.1 96.5 %copy-start.6 = (f32[2048]{0:T(1024)S(1)}, f32[2048]{0:T(1024)}, u32[]{:S(2)}) copy-start(f32[2048]{0:T(1024)} %param.21) | copy-start | bytes 24580
  322.5 0.8 copy-start.4
Sparse Core Ops, SparseCore 0:
  10.1 43.3 all-gather.4
  55.6 52.1 all-gather.2

commit v2 on v0

v2 whole, which is shorter than its diff:
```python
import jax
import jax.numpy as jnp
from jax import lax
from jax.experimental import pallas as pl
from jax.experimental.pallas import tpu as pltpu
from jax.sharding import PartitionSpec as P

NX, NZ, NY, NC = 4, 16, 4, 2
NDP = NY * NC
ROWS, D, FB, FF, TOP, CAP = 32, 2048, 512, 768, 8, 8
GU_ROWS, DN_COLS, CUT = D // NDP, D // NDP, 192
PAIRS = NZ // 2
MESH = pl.DeviceIdType.MESH
F32, BF16 = jnp.float32, jnp.bfloat16
NT = (((1,), (1,)), ((), ()))


def remote(src, dst, send_sem, recv_sem, peer):
    return pltpu.make_async_remote_copy(
        src_ref=src,
        dst_ref=dst,
        send_sem=send_sem,
        recv_sem=recv_sem,
        device_id=peer,
        device_id_type=MESH,
    )


def ring_steps(h):
    return [side for side in (0, 1) if (side == 0 and h <= 7) or (side == 1 and h >= 1)]


def kernel(
    attn_ref,
    resid_ref,
    w_ref,
    gain_post_ref,
    ids_ref,
    logits_ref,
    live_ref,
    gate_up_ref,
    down_ref,
    gain_final_ref,
    stream_ref,
    normed_ref,
    wbuf,
    pbuf,
    rbuf,
    held,
    zbuf,
    cbuf,
    xbuf,
    inner,
    ybuf,
    ret,
    part,
    up_out,
    up_in,
    dn_out,
    dn_in,
    gu,
    dn,
    wz_send,
    wz_recv,
    wx_send,
    wx_recv,
    rs_send,
    rs_recv,
    own_sem,
    wt_send,
    wt_recv,
    nz_send,
    nz_recv,
    cx_send,
    cx_recv,
    yx_send,
    yx_recv,
    up_send,
    up_recv,
    dn_send,
    dn_recv,
):
    dp = lax.axis_index("dp")
    expert = lax.axis_index("expert")
    x, z = expert // NZ, expert % NZ
    y, core = dp // NC, dp % NC
    above, below = (dp, x * NZ + (z + 1) % NZ), (dp, x * NZ + (z + NZ - 1) % NZ)
    xpeer = [(dp, (x + step) % NX * NZ + z) for step in range(NX)]
    right, left = xpeer[1], xpeer[3]

    peers = [above, below] + xpeer[1:] + [((dp + step) % NDP, expert) for step in range(1, NDP)]
    barrier = pltpu.get_barrier_semaphore()
    for peer in peers:
        pl.semaphore_signal(barrier, inc=1, device_id=peer, device_id_type=MESH)
    pl.semaphore_wait(barrier, len(peers))

    wbuf[expert] = w_ref[...]

    def z_at(side, h):
        return (z + (h if side == 0 else NZ - h)) % NZ

    def w_block(column, side, h):
        return wbuf.at[(x + column) % NX * NZ + z_at(side, h)]

    def ring_copy(ref, side, h, send, recv):
        at = side * 8 + h
        return remote(ref, ref, send.at[at], recv.at[at], below if side == 0 else above)

    def wz_copy(side, h):
        return ring_copy(w_block(0, side, h), side, h, wz_send, wz_recv)

    def wz_arrival(side, h):
        return ring_copy(w_block(0, side, h), side, h - 1, wz_send, wz_recv)

    def place(side, h):
        return h if side == 0 else 7 + h

    def wx_copy(way, side, h):
        at = way * 16 + place(side, h)
        column = 0 if way < 2 else (1 if side == 0 else 3)
        peer = (right, left, left if side == 0 else right)[way]
        ref = w_block(column, side, h)
        return remote(ref, ref, wx_send.at[at], wx_recv.at[at], peer)

    def wx_arrival(way, side, h):
        at = way * 16 + place(side, h)
        ref = w_block((3, 1, 2)[way], side, h)
        return remote(ref, ref, wx_send.at[at], wx_recv.at[at], right)

    def w_forward(h):
        for side in ring_steps(h):
            wx_arrival(1 if side == 0 else 0, side, h).wait_recv()
            wx_copy(2, side, h).start()

    wz_copy(0, 0).start()
    wz_copy(1, 0).start()
    wx_copy(0, 0, 0).start()
    wx_copy(1, 0, 0).start()

    y_up, y_down = ((y + 1) % NY * NC + core, expert), ((y + NY - 1) % NY * NC + core, expert)
    sibling = (y * NC + 1 - core, expert)

    def piece(owner, number):
        if number == 2:
            return dn.at[owner]
        begin = pl.multiple_of(owner * GU_ROWS, GU_ROWS)
        return gu.at[pl.ds(begin, CUT)] if number == 0 else gu.at[pl.ds(begin + CUT, GU_ROWS - CUT)]

    def own_piece(number):
        if number == 2:
            return down_ref
        return gate_up_ref.at[pl.ds(0, CUT)] if number == 0 else gate_up_ref.at[pl.ds(CUT, GU_ROWS - CUT)]

    def owner_of(step, on_core):
        return (y + step) % NY * NC + on_core

    def wt(kind, number, src, dst, peer):
        at = kind * 3 + number
        return remote(src, dst, wt_send.at[at], wt_recv.at[at], peer)

    def weight_send(kind, number):
        if kind in (0, 1, 3):
            peer = {0: y_up, 1: y_down, 3: sibling}[kind]
            return wt(kind, number, own_piece(number), piece(dp, number), peer)
        if kind == 2:
            owner = owner_of(3 if number == 0 else 1, core)
            ref = piece(owner, number)
            return wt(kind, number, ref, ref, y_up if number == 0 else y_down)
        ref = piece(owner_of({4: 3, 5: 1, 6: 2}[kind], core), number)
        return wt(kind, number, ref, ref, sibling)

    def weight_arrival(kind, number):
        owner = {
            0: owner_of(3, core),
            1: owner_of(1, core),
            2: owner_of(2, core),
            3: owner_of(0, 1 - core),
            4: owner_of(3, 1 - core),
            5: owner_of(1, 1 - core),
            6: owner_of(2, 1 - core),
        }[kind]
        ref = piece(owner, number)
        return wt(kind, number, ref, ref, sibling)

    def own_copy(number):
        return pltpu.make_async_copy(own_piece(number), piece(dp, number), own_sem.at[number])

    for number in range(3):
        weight_send(0, number).start()
        weight_send(1, 2 - number).start()
    for number in range(3):
        weight_send(3, number).start()
        own_copy(number).start()

    lane = lax.broadcasted_iota(jnp.int32, (NZ, 128), 1)
    named = lane // ROWS * NZ + lax.broadcasted_iota(jnp.int32, (NZ, 128), 0)
    logits = logits_ref[...]
    raised = jnp.exp(logits - jnp.max(logits, axis=0, keepdims=True))
    probs = (raised / jnp.sum(raised, axis=0, keepdims=True)).astype(BF16).astype(F32)
    chosen = jnp.zeros((NZ, 128), F32)
    weight = jnp.zeros((NZ, 128), F32)
    for k in range(TOP):
        same = named == ids_ref[k : k + 1, :]
        chosen += jnp.where(same, 1.0, 0.0)
        weight += jnp.where(same, probs[k : k + 1, :], 0.0)
    chosen = jnp.where(lane % ROWS < live_ref[...], chosen, 0.0)
    row_l = lax.broadcasted_iota(jnp.int32, (128, 128), 0)
    col_l = lax.broadcasted_iota(jnp.int32, (128, 128), 1)
    before = jnp.where((row_l // ROWS == col_l // ROWS) & (row_l < col_l), 1.0, 0.0).astype(BF16)
    rank = jnp.dot(chosen.astype(BF16), before, preferred_element_type=F32)
    slots = jnp.where(chosen > 0.5, rank, -1.0)
    zbuf[z, 0:NZ, D:] = slots.astype(BF16)
    zbuf[z, NZ:, D:] = weight.astype(BF16)

    for h in range(1, 9):
        for side in ring_steps(h):
            wz_arrival(side, h).wait_recv()
            if h < (7 if side == 0 else 8):
                wz_copy(side, h).start()
            wx_copy(0, side, h).start()
            wx_copy(1, side, h).start()
        if h >= 2:
            w_forward(h - 2)
    w_forward(7)
    w_forward(8)
    every = [(side, h) for h in range(9) for side in ring_steps(h)]

    def rs_copy(step, order):
        column = (x + (0, 3, 1, 2)[order]) % NX
        target = (dp + step) % NDP
        at = (step - 1) * 4 + order
        return remote(
            pbuf.at[column, target], rbuf.at[dp, column], rs_send.at[at], rs_recv.at[at], (target, expert)
        )

    def rs_arrival(step, order):
        column = (x + (0, 3, 1, 2)[order]) % NX
        source = (dp + NDP - step) % NDP
        at = (step - 1) * 4 + order
        return remote(
            pbuf.at[column, source], rbuf.at[source, column], rs_send.at[at], rs_recv.at[at], (source, expert)
        )

    for order in range(4):
        column = (x + (0, 3, 1, 2)[order]) % NX
        if order:
            for side, h in every:
                if (order - 1, side) not in ((0, 1), (1, 0)):
                    wx_arrival(order - 1, side, h).wait_recv()
        block = wbuf[pl.ds(column * NZ, NZ)].reshape(FB, FB)
        got = lax.dot_general(attn_ref[...], block, NT, preferred_element_type=F32)
        pbuf[column] = got.astype(BF16).reshape(NDP, ROWS, FB)
        for step in range(1, NDP):
            rs_copy(step, order).start()

    for number in range(3):
        weight_arrival(0, number).wait_recv()
        weight_arrival(1, 2 - number).wait_recv()
        if number == 0:
            weight_send(2, 0).start()
            weight_send(2, 2).start()
        if number == 1:
            weight_send(2, 1).start()
    for number in range(3):
        weight_send(4, number).start()
        weight_send(5, number).start()

    for order in range(4):
        column = (x + (0, 3, 1, 2)[order]) % NX
        for step in range(1, NDP):
            rs_arrival(step, order).wait_recv()
        rbuf[dp, column] = pbuf[column, dp]

    square = jnp.zeros((ROWS, 1), F32)
    for g in range(4):
        cols = slice(g * FB, (g + 1) * FB)
        proj = rbuf[0, g].astype(F32)
        for source in range(1, NDP):
            proj += rbuf[source, g].astype(F32)
        both = (resid_ref[:, cols].astype(F32) + proj).astype(BF16)
        held[:, cols] = both
        wide = both.astype(F32)
        square += jnp.sum(wide * wide, axis=-1, keepdims=True)
    scale = lax.rsqrt(square / D + 1e-06)
    zbuf[z, :, 0:D] = (held[...].astype(F32) * scale * gain_post_ref[...]).astype(BF16)

    def nz_copy(side, h):
        return ring_copy(zbuf.at[z_at(side, h)], side, h, nz_send, nz_recv)

    def nz_arrival(side, h):
        return ring_copy(zbuf.at[z_at(side, h)], side, h - 1, nz_send, nz_recv)

    nz_copy(0, 0).start()
    nz_copy(1, 0).start()

    slot_i = lax.broadcasted_iota(jnp.int32, (64, 128), 0)
    slot_l = lax.broadcasted_iota(jnp.int32, (64, 128), 1)
    slot_k = (slot_i % CAP).astype(F32)
    slot_x = slot_l // ROWS == slot_i // 16
    slot_side = [slot_x & (slot_i // CAP % 2 == side) for side in range(2)]
    fold = jnp.where(
        lax.broadcasted_iota(jnp.int32, (ROWS, 128), 1) % ROWS == lax.broadcasted_iota(jnp.int32, (ROWS, 128), 0), 1.0, 0.0
    ).astype(BF16)
    here = lax.broadcasted_iota(jnp.int32, (NZ, 128), 0) == z

    def table_row(source, begin):
        table = zbuf[source, begin : begin + NZ, D:].astype(F32)
        return jnp.sum(jnp.where(here, table, 0.0), axis=0, keepdims=True)

    def pair_sources(h):
        return (z_at(0, h), z_at(1, h)) if h < PAIRS else (z, z_at(1, h))

    def hits(source, side):
        return slot_side[side] & (table_row(source, 0) == slot_k)

    def compact(h):
        total = jnp.zeros((64, D), F32)
        for side, source in enumerate(pair_sources(h)):
            picked = jnp.where(hits(source, side), 1.0, 0.0).astype(BF16)
            choose = lax.dot_general(picked, fold, NT, preferred_element_type=F32).astype(BF16)
            total += jnp.dot(choose, zbuf[source, :, 0:D], preferred_element_type=F32)
        cbuf[h - 1] = total.astype(BF16).reshape(NX, 16, D)

    def cx_copy(h, step):
        at = (h - 1) * 3 + step - 1
        target = (x + step) % NX
        return remote(cbuf.at[h - 1, target], xbuf.at[h - 1, x], cx_send.at[at], cx_recv.at[at], xpeer[step])

    def cx_arrival(h, step):
        at = (h - 1) * 3 + step - 1
        source = (x + NX - step) % NX
        return remote(
            cbuf.at[h - 1, source], xbuf.at[h - 1, source], cx_send.at[at], cx_recv.at[at], xpeer[NX - step]
        )

    def yx_copy(h, step):
        at = (h - 1) * 3 + step - 1
        target = (x + step) % NX
        return remote(ybuf.at[h - 1, target], ret.at[h - 1, x], yx_send.at[at], yx_recv.at[at], xpeer[step])

    def yx_arrival(h, step):
        at = (h - 1) * 3 + step - 1
        source = (x + NX - step) % NX
        return remote(
            ybuf.at[h - 1, source], ret.at[h - 1, source], yx_send.at[at], yx_recv.at[at], xpeer[NX - step]
        )

    def expert_first(chunk):
        for h in (2 * chunk + 1, 2 * chunk + 2):
            for step in range(1, NX):
                cx_arrival(h, step).wait_recv()

        def columns(n, carry):
            rows_in = xbuf[2 * chunk : 2 * chunk + 2].reshape(128, D)
            begin = pl.multiple_of(n * 256, 256)
            gate = jnp.dot(rows_in, gu[:, pl.ds(begin, 256)], preferred_element_type=F32)
            up = jnp.dot(rows_in, gu[:, pl.ds(FF + begin, 256)], preferred_element_type=F32)
            inner[:, pl.ds(begin, 256)] = (gate / (1.0 + jnp.exp(-gate)) * up).astype(BF16)
            return carry

        lax.fori_loop(0, FF // 256, columns, 0)

    def expert_second(chunk):
        def columns(n, carry):
            begin = pl.multiple_of(n * DN_COLS, DN_COLS)
            out = jnp.dot(inner[...], dn[n], preferred_element_type=F32)
            ybuf[2 * chunk : 2 * chunk + 2, :, :, pl.ds(begin, DN_COLS)] = out.astype(BF16).reshape(2, NX, 16, DN_COLS)
            return carry

        lax.fori_loop(0, NDP, columns, 0)
        for h in (2 * chunk + 2, 2 * chunk + 1):
            for step in (2, 1, 3):
                yx_copy(h, step).start()
            ret[h - 1, x] = ybuf[h - 1, x]

    for h in range(1, PAIRS + 1):
        for side in ring_steps(h):
            nz_arrival(side, h).wait_recv()
            if h < (7 if side == 0 else 8):
                nz_copy(side, h).start()
        compact(h)
        for step in (2, 1, 3):
            cx_copy(h, step).start()
        xbuf[h - 1, x] = cbuf[h - 1, x]
        if h == 1:
            for number in range(3):
                weight_arrival(2, number).wait_recv()
                weight_send(6, number).start()
        if h == 3:
            for kind in (3, 4, 5, 6):
                for number in range(3):
                    weight_arrival(kind, number).wait_recv()
            for number in range(3):
                own_copy(number).wait()
        if h >= 3:
            (expert_first if h % 2 else expert_second)((h - 3) // 2)
    expert_first(3)
    expert_second(3)

    def partial_sum(h, side):
        source = pair_sources(h)[side]
        scaled = jnp.where(hits(source, side), table_row(source, NZ), 0.0).astype(BF16)
        spread = lax.dot_general(fold, scaled, NT, preferred_element_type=F32).astype(BF16)
        return jnp.dot(spread, ret[h - 1].reshape(64, D), preferred_element_type=F32)

    for h in range(1, PAIRS + 1):
        if h == 7:
            continue
        for step in range(1, NX):
            yx_arrival(h, step).wait_recv()
        for side in range(2):
            part[h - 1, side] = partial_sum(h, side)
    def up_copy(t):
        return remote(up_out.at[t], up_in.at[t], up_send.at[t], up_recv.at[t], above)

    def dn_copy(t):
        return remote(dn_out.at[t], dn_in.at[t], dn_send.at[t], dn_recv.at[t], below)

    up_out[0] = part[7, 1].astype(BF16)
    up_copy(0).start()
    for step in range(1, NX):
        yx_arrival(7, step).wait_recv()
    dn_out[0] = partial_sum(7, 1).astype(BF16)
    dn_copy(0).start()
    part[6, 0] = partial_sum(7, 0)
    for t in range(1, 8):
        up_copy(t - 1).wait_recv()
        up_out[t] = (up_in[t - 1].astype(F32) + part[7 - t, 0]).astype(BF16)
        up_copy(t).start()
        if t < 7:
            dn_copy(t - 1).wait_recv()
            dn_out[t] = (dn_in[t - 1].astype(F32) + part[6 - t, 1]).astype(BF16)
            dn_copy(t).start()
    total = held[...].astype(F32) + part[7, 0]
    dn_copy(6).wait_recv()
    total += dn_in[6].astype(F32)
    up_copy(7).wait_recv()
    final = (total + up_in[7].astype(F32)).astype(BF16)
    stream_ref[...] = final
    wide = final.astype(F32)
    scale = lax.rsqrt(jnp.mean(wide * wide, axis=-1, keepdims=True) + 1e-06)
    normed_ref[...] = (wide * scale * gain_final_ref[...]).astype(BF16)

    for side, h in every + [(1, 0)]:
        if h < (7 if side == 0 else 8):
            wz_copy(side, h).wait_send()
            nz_copy(side, h).wait_send()
    for side, h in every:
        for way in range(3):
            wx_copy(way, side, h).wait_send()
    for order in range(4):
        for step in range(1, NDP):
            rs_copy(step, order).wait_send()
    for kind in range(7):
        for number in range(3):
            weight_send(kind, number).wait_send()
    for h in range(1, PAIRS + 1):
        for step in range(1, NX):
            cx_copy(h, step).wait_send()
            yx_copy(h, step).wait_send()
    for t in range(8):
        up_copy(t).wait_send()
        if t < 7:
            dn_copy(t).wait_send()


def block(*args):
    vmem = pl.BlockSpec(memory_space=pltpu.VMEM)
    hbm = pl.BlockSpec(memory_space=pl.ANY)
    dma = pltpu.SemaphoreType.DMA
    return pl.pallas_call(
        kernel,
        out_shape=[jax.ShapeDtypeStruct((ROWS, D), BF16)] * 2,
        in_specs=[vmem] * 7 + [hbm] * 2 + [vmem],
        out_specs=[vmem] * 2,
        scratch_shapes=[
            pltpu.VMEM((NX * NZ, ROWS, FB), BF16),
            pltpu.VMEM((NX, NDP, ROWS, FB), BF16),
            pltpu.VMEM((NDP, NX, ROWS, FB), BF16),
            pltpu.VMEM((ROWS, D), BF16),
            pltpu.VMEM((NZ, ROWS, D + 128), BF16),
            pltpu.VMEM((PAIRS, NX, 16, D), BF16),
            pltpu.VMEM((PAIRS, NX, 16, D), BF16),
            pltpu.VMEM((128, FF), BF16),
            pltpu.VMEM((PAIRS, NX, 16, D), BF16),
            pltpu.VMEM((PAIRS, NX, 16, D), BF16),
            pltpu.VMEM((PAIRS, 2, ROWS, D), F32),
            pltpu.VMEM((8, ROWS, D), BF16),
            pltpu.VMEM((8, ROWS, D), BF16),
            pltpu.VMEM((7, ROWS, D), BF16),
            pltpu.VMEM((7, ROWS, D), BF16),
            pltpu.VMEM((D, 2 * FF), BF16),
            pltpu.VMEM((NDP, FF, DN_COLS), BF16),
            dma((16,)),
            dma((16,)),
            dma((48,)),
            dma((48,)),
            dma((28,)),
            dma((28,)),
            dma((3,)),
            dma((21,)),
            dma((21,)),
            dma((16,)),
            dma((16,)),
            dma((24,)),
            dma((24,)),
            dma((24,)),
            dma((24,)),
            dma((8,)),
            dma((8,)),
            dma((7,)),
            dma((7,)),
        ],
        compiler_params=pltpu.CompilerParams(
            collective_id=0, has_side_effects=True, vmem_limit_bytes=56 << 20
        ),
    )(*args)


def body(
    attn,
    resid,
    w_out,
    gain_post,
    route_ids,
    route_logits,
    live_count,
    w_gate_up,
    w_down,
    gain_final,
):
    ids = jnp.tile(route_ids[0].T, (1, NX))
    logits = jnp.tile(route_logits[0].T, (1, NX))
    live = jnp.broadcast_to(live_count, (1, 128))
    stream_out, normed_out = block(
        attn[0],
        resid[0],
        w_out.T,
        gain_post[None],
        ids,
        logits,
        live,
        w_gate_up[0],
        w_down[0],
        gain_final[None],
    )
    return (stream_out[None], normed_out[None])


def solution(mesh):
    placed = (
        P("expert", None, "dp"),
        P("expert", "dp", None),
        P("dp", "expert"),
        P(),
        P("expert", "dp", None),
        P("expert", "dp", None),
        P("expert", "dp"),
        P("expert", "dp", None),
        P("expert", None, "dp"),
        P(),
    )
    return jax.shard_map(
        body,
        mesh=mesh,
        in_specs=placed,
        out_specs=(P("expert", "dp", None), P("expert", "dp", None)),
        check_vma=False,
    )
```

time: 446 us -> 161 us (0.36)
  the two profiles are of different devices: /device:TPU:62 before, /device:TPU:96 now
where the time goes in v2:
time: 161 us; the launch traced here: 160 us
  Pallas kernels  154 us (96%)
  local copies, waits for them, and re-layouts  4.91 us (3%)
    pallas_call x1, Pallas kernels, block(): pl.pallas_call(kernel, out_shape=[jax.ShapeDtypeStruct((ROWS, D), BF16)]...  154 us

profile of v2, /device:TPU:96, one launch (start us, length us, event | category | flops | bytes accessed | tf_op | source)
XLA Modules:
  0.0 160.4 jit_solution(10369222205715425917)
XLA Ops:
  1.3 0.6 broadcast_in_dim.21.live_ref
  1.9 0.0 copy-start.1
  1.9 0.7 copy-done.1
  2.6 0.0 copy-start.2
  2.6 0.7 tile.9.ids_ref
  3.2 0.0 copy-done.2
  3.2 0.7 tile.21.logits_ref
  3.9 154.2 %shard_map.113 = (bf16[32,2048]{1,0:T(8,128)(2,1)}, bf16[32,2048]{1,0:T(8,128)(2,1)}) custom-call(bf16[256,512]{1,0:T(8,128)(2,1)} %bitcast.19, bf16[32,2048]{1,0:T(8,128)(2,1)} %bitcast.20, bf16[32,512]{1,0:T(8,128)(2,1)} %bitcast.23, f32[1,2048]{1,0:T(1,128)} %bitcast.24, s32[8,128]{1,0:T(8,128)} %tile.9.ids_ref, f32[8,128]{1,0:T(8,128)} %tile.21.logits_ref, ...), custom_call_target="tpu_custom_call" | custom-call | tf_op jit(solution)/shard_map/pallas_call | solution.py:471
  158.1 0.0 copy-start
  158.1 1.6 copy.15
  159.7 0.0 copy-done
  159.7 0.7 copy.16
  (2 shorter events, 0.0 us)
Async XLA Ops:
  1.9 0.7 copy-start.1
  2.6 0.7 copy-start.2
  158.1 1.6 %copy-start = (bf16[32,2048]{1,0:T(8,128)(2,1)S(1)}, bf16[32,2048]{1,0:T(8,128)(2,1)}, u32[]{:S(2)}) copy-start(bf16[32,2048]{1,0:T(8,128)(2,1)} %get-tuple-element.5) | copy-start | bytes 393220

commit v3 on v0

v3 whole, which is shorter than its diff:
```python
import jax
import jax.numpy as jnp
from jax import lax
from jax.experimental import pallas as pl
from jax.experimental.pallas import tpu as pltpu
from jax.sharding import PartitionSpec as P

NX, NZ, NY, NC = 4, 16, 4, 2
NDP = NY * NC
ROWS, D, FB, FF, TOP, CAP = 32, 2048, 512, 768, 8, 8
GU_ROWS, DN_COLS, CUT = D // NDP, D // NDP, 192
PAIRS = NZ // 2
MESH = pl.DeviceIdType.MESH
F32, BF16 = jnp.float32, jnp.bfloat16
NT = (((1,), (1,)), ((), ()))


def remote(src, dst, send_sem, recv_sem, peer):
    return pltpu.make_async_remote_copy(
        src_ref=src,
        dst_ref=dst,
        send_sem=send_sem,
        recv_sem=recv_sem,
        device_id=peer,
        device_id_type=MESH,
    )


def kernel(
    attn_ref,
    resid_ref,
    w_ref,
    gain_post_ref,
    ids_ref,
    logits_ref,
    live_ref,
    gate_up_ref,
    down_ref,
    gain_final_ref,
    stream_ref,
    normed_ref,
    abuf,
    resid,
    wbuf,
    pbuf,
    rbuf,
    sums_out,
    sums_in,
    sums,
    held,
    zbuf,
    cbuf,
    xbuf,
    cmat,
    inner,
    ybuf,
    ret,
    part,
    up_out,
    up_in,
    dn_out,
    dn_in,
    gu,
    dn,
    own_sem,
    sent,
    w_recv,
    a_recv,
    rs_recv,
    sx_recv,
    near_recv,
    far_recv,
    sib_recv,
    nz_recv,
    cx_recv,
    yx_recv,
    up_recv,
    dn_recv,
):
    dp = lax.axis_index("dp")
    expert = lax.axis_index("expert")
    x, z = expert // NZ, expert % NZ
    y, core = dp // NC, dp % NC
    zpeer = {step: (dp, x * NZ + (z + NZ + step) % NZ) for step in (-2, -1, 1, 2)}
    above, below = zpeer[1], zpeer[-1]

    def xpeer(step):
        return (dp, (x + step) % NX * NZ + z)

    right, left = xpeer(1), xpeer(3)
    y_up, y_down = ((y + 1) % NY * NC + core, expert), ((y + NY - 1) % NY * NC + core, expert)
    sibling = (y * NC + 1 - core, expert)

    W, A, RS, SX, GU, DN, NZS, CX, YX, UP, DOWN = range(11)

    def left_all(kind, ref):
        remote(ref, ref, sent.at[kind], rs_recv.at[0], right).wait_send()

    def arrived(ref, semaphore):
        remote(ref, ref, sent.at[0], semaphore, right).wait_recv()

    def local(src, dst, at):
        return pltpu.make_async_copy(src, dst, own_sem.at[at])

    attn_in = local(attn_ref, abuf.at[x], 3)
    resid_in = local(resid_ref, resid, 4)
    attn_in.start()
    resid_in.start()
    same = lax.broadcasted_iota(jnp.int32, (ROWS, ROWS), 0) == lax.broadcasted_iota(jnp.int32, (ROWS, ROWS), 1)
    eye = jnp.where(same, 1.0, 0.0).astype(BF16)
    wbuf[z] = lax.dot_general(eye, w_ref[...], NT, preferred_element_type=F32).astype(BF16)

    peers = list(zpeer.values()) + [xpeer(step) for step in range(1, NX)]
    peers += [((dp + step) % NDP, expert) for step in range(1, NDP)]
    barrier = pltpu.get_barrier_semaphore()
    for peer in peers:
        pl.semaphore_signal(barrier, inc=1, device_id=peer, device_id_type=MESH)
    pl.semaphore_wait(barrier, len(peers))

    def z_at(side, h):
        return (z + (h if side == 0 else NZ - h)) % NZ

    def w_copy(side, h):
        ref = wbuf.at[z_at(side, max(h - 2, 0))]
        step = (1 if side else -1) * min(h, 2)
        return remote(ref, ref, sent.at[W], w_recv.at[side * 8 + h - 1], zpeer[step])

    def half_rows(half):
        return pl.ds(half * 128, 128)

    def a_copy(way, half):
        if way < 2:
            src, dst = attn_ref.at[half_rows(half)], abuf.at[x, half_rows(half)]
        else:
            src = dst = abuf.at[(x + (3, 1)[half]) % NX, half_rows(half)]
        peer = (right, left)[way if way < 2 else half]
        return remote(src, dst, sent.at[A], a_recv.at[way * 2 + half], peer)

    def a_arrived(way, half):
        arrived(abuf.at[(x + (3, 1, 2)[way]) % NX, half_rows(half)], a_recv.at[way * 2 + half])

    for h in (1, 2):
        w_copy(1, h).start()
        w_copy(0, h).start()
    for half in range(2):
        a_copy(0, half).start()
        a_copy(1, 1 - half).start()

    def piece(owner, number):
        if number == 2:
            return dn.at[owner]
        begin = pl.multiple_of(owner * GU_ROWS, GU_ROWS)
        return gu.at[pl.ds(begin, CUT)] if number == 0 else gu.at[pl.ds(begin + CUT, GU_ROWS - CUT)]

    def own_piece(number):
        if number == 2:
            return down_ref
        return gate_up_ref.at[pl.ds(0, CUT)] if number == 0 else gate_up_ref.at[pl.ds(CUT, GU_ROWS - CUT)]

    def owner_of(step, on_core):
        return (y + step) % NY * NC + on_core

    def weight_copy(src, dst, number, recv, peer):
        return remote(src, dst, sent.at[DN if number == 2 else GU], recv, peer)

    def to_near(side, number):
        peer = (y_up, y_down)[side]
        return weight_copy(own_piece(number), piece(dp, number), number, near_recv.at[side * 3 + number], peer)

    def near_arrived(side, number):
        arrived(piece(owner_of((3, 1)[side], core), number), near_recv.at[side * 3 + number])

    def to_far(number):
        ref = piece(owner_of(3 if number == 0 else 1, core), number)
        return weight_copy(ref, ref, number, far_recv.at[number], y_up if number == 0 else y_down)

    def to_sibling(step, number):
        recv = sib_recv.at[1 if number == 2 else 0]
        owner = owner_of(step, core)
        src = piece(owner, number) if step else own_piece(number)
        return weight_copy(src, piece(owner, number), number, recv, sibling)

    def own_copy(number):
        return local(own_piece(number), piece(dp, number), number)

    for number in range(3):
        to_near(0, number).start()
        to_near(1, 2 - number).start()
    for number in range(3):
        to_sibling(0, number).start()
        own_copy(number).start()

    logits = logits_ref[...]
    raised = jnp.exp(logits - jnp.max(logits, axis=1, keepdims=True))
    probs = (raised / jnp.sum(raised, axis=1, keepdims=True)).astype(BF16)
    fold = jnp.where(
        lax.broadcasted_iota(jnp.int32, (ROWS, 128), 1) % ROWS == lax.broadcasted_iota(jnp.int32, (ROWS, 128), 0), 1.0, 0.0
    ).astype(BF16)
    ids = ids_ref[...].astype(F32).astype(BF16)
    ids_t = lax.dot_general(ids, fold, (((0,), (0,)), ((), ())), preferred_element_type=F32)
    probs_t = lax.dot_general(probs, fold, (((0,), (0,)), ((), ())), preferred_element_type=F32)
    lane = lax.broadcasted_iota(jnp.int32, (NZ, 128), 1)
    named = (lane // ROWS * NZ + lax.broadcasted_iota(jnp.int32, (NZ, 128), 0)).astype(F32)
    chosen = jnp.zeros((NZ, 128), F32)
    weight = jnp.zeros((NZ, 128), F32)
    for k in range(TOP):
        found = named == ids_t[k : k + 1, :]
        chosen += jnp.where(found, 1.0, 0.0)
        weight += jnp.where(found, probs_t[k : k + 1, :], 0.0)
    chosen = jnp.where(lane % ROWS < live_ref[...], chosen, 0.0)
    row_l = lax.broadcasted_iota(jnp.int32, (128, 128), 0)
    col_l = lax.broadcasted_iota(jnp.int32, (128, 128), 1)
    before = jnp.where((row_l // ROWS == col_l // ROWS) & (row_l < col_l), 1.0, 0.0).astype(BF16)
    rank = jnp.dot(chosen.astype(BF16), before, preferred_element_type=F32)
    zbuf[z, 0, :, D:] = jnp.where(chosen > 0.5, rank, -1.0).astype(BF16)
    zbuf[z, 1, :, D:] = weight.astype(BF16)

    for h in range(1, 9):
        for side in (1, 0):
            if h <= 7 + side:
                arrived(wbuf.at[z_at(side, h)], w_recv.at[side * 8 + h - 1])
                if h + 2 <= 7 + side:
                    w_copy(side, h + 2).start()
        if h == 2:
            a_arrived(0, 0)
            a_copy(2, 0).start()
            a_arrived(1, 1)
            a_copy(2, 1).start()
    attn_in.wait()
    resid_in.wait()
    for way, half in ((0, 1), (1, 0), (2, 0), (2, 1)):
        a_arrived(way, half)

    def product(order, carry):
        got = lax.dot_general(
            abuf[(x + 3 - order) % NX], wbuf[...].reshape(FB, FB), NT, preferred_element_type=F32
        )
        pbuf[:, order] = got.astype(BF16).reshape(NDP, ROWS, FB)

        @pl.when(order % 2 == 1)
        def _():
            pair = pl.ds(order - 1, 2)
            for step in (4, 3, 5, 2, 6, 1, 7):
                target = (dp + step) % NDP
                remote(
                    pbuf.at[target, pair], rbuf.at[dp, pair], sent.at[RS], rs_recv.at[order // 2], (target, expert)
                ).start()

        return carry

    lax.fori_loop(0, NX, product, 0)

    def sum_up(order, carry):
        @pl.when(order % 2 == 0)
        def _():
            arrived(rbuf.at[pl.ds(0, 7), pl.ds(0, 2)], rs_recv.at[order // 2])

        total = pbuf[dp, order].astype(F32)
        for step in range(1, NDP):
            total += rbuf[(dp + step) % NDP, order].astype(F32)

        @pl.when(order < 3)
        def _():
            sums_out[order] = total.astype(BF16)
            remote(sums_out.at[order], sums_in.at[x], sent.at[SX], sx_recv.at[0], xpeer(3 - order)).start()

        @pl.when(order == 3)
        def _():
            sums[x] = total

        return carry

    lax.fori_loop(0, NX, sum_up, 0)

    for number in range(3):
        near_arrived(0, number)
        near_arrived(1, 2 - number)
        if number == 0:
            to_far(0).start()
            to_far(2).start()
        if number == 1:
            to_far(1).start()
    for number in range(3):
        to_sibling(3, number).start()
        to_sibling(1, number).start()

    arrived(sums_in.at[pl.ds(0, 3)], sx_recv.at[0])
    for step in range(1, NX):
        source = (x + step) % NX
        sums[source] = sums_in[source].astype(F32)

    square = jnp.zeros((ROWS, 1), F32)
    for g in range(4):
        cols = slice(g * FB, (g + 1) * FB)
        both = (resid[:, cols].astype(F32) + sums[g]).astype(BF16)
        held[:, cols] = both
        wide = both.astype(F32)
        square += jnp.sum(wide * wide, axis=-1, keepdims=True)
    scale = lax.rsqrt(square / D + 1e-06)
    normed = (held[...].astype(F32) * scale * gain_post_ref[...]).astype(BF16)
    zbuf[z, :, :, 0:D] = normed.reshape(2, 16, D)

    def nz_copy(side, h, half):
        ref = zbuf.at[z_at(side, h), half]
        return remote(ref, ref, sent.at[NZS], nz_recv.at[(side * 8 + h) * 2 + half], above if side else below)

    for half in range(2):
        nz_copy(1, 0, half).start()
        nz_copy(0, 0, half).start()

    slot_i = lax.broadcasted_iota(jnp.int32, (64, 128), 0)
    slot_l = lax.broadcasted_iota(jnp.int32, (64, 128), 1)
    slot_k = (slot_i % CAP).astype(F32)
    slot_x = slot_l // ROWS == slot_i // 16
    slot_side = [slot_x & (slot_i // CAP % 2 == side) for side in range(2)]
    here = lax.broadcasted_iota(jnp.int32, (NZ, 128), 0) == z

    def table_row(source, half):
        table = zbuf[source, half, :, D:].astype(F32)
        return jnp.sum(jnp.where(here, table, 0.0), axis=0, keepdims=True)

    def compact(h):
        total = jnp.zeros((64, D), F32)
        for side, source in enumerate((z_at(0, h % PAIRS), z_at(1, h))):
            hit = slot_side[side] & (table_row(source, 0) == slot_k)
            picked = jnp.where(hit, 1.0, 0.0).astype(BF16)
            choose = lax.dot_general(picked, fold, NT, preferred_element_type=F32).astype(BF16)
            scaled = jnp.where(hit, table_row(source, 1), 0.0).astype(BF16)
            spread = lax.dot_general(fold, scaled, NT, preferred_element_type=F32)
            cmat[h - 1, side * ROWS : (side + 1) * ROWS] = spread.astype(BF16)
            total += jnp.dot(choose, zbuf[source, :, :, 0:D].reshape(ROWS, D), preferred_element_type=F32)
        cbuf[h - 1] = total.astype(BF16).reshape(NX, 16, D)
        for step in (2, 1, 3):
            target = (x + step) % NX
            remote(
                cbuf.at[h - 1, target], xbuf.at[h - 1, x], sent.at[CX], cx_recv.at[h - 1], xpeer(step)
            ).start()
        xbuf[h - 1, x] = cbuf[h - 1, x]

    def ring_step(h, carry):
        for half in range(2):
            for side in (1, 0):

                @pl.when(h <= 7 + side)
                def _():
                    arrived(zbuf.at[z_at(side, h), half], nz_recv.at[(side * 8 + h - 1) * 2 + half])

                @pl.when(h < 7 + side)
                def _():
                    nz_copy(side, h, half).start()


        @pl.when(h == 7)
        def _():
            for number in range(3):
                arrived(piece(owner_of(2, core), number), far_recv.at[number])
                to_sibling(2, number).start()

        compact(h)
        return carry

    lax.fori_loop(1, PAIRS + 1, ring_step, 0)

    arrived(gu.at[pl.ds(0, 4 * GU_ROWS)], sib_recv.at[0])
    arrived(dn.at[pl.ds(0, 4)], sib_recv.at[1])
    for number in range(3):
        own_copy(number).wait()

    def chunk_step(order, carry):
        begin = (1 - order) * 4
        for pair in range(4):
            arrived(xbuf.at[begin + pair, pl.ds(0, 3)], cx_recv.at[begin + pair])

        def hidden(n, carry):
            rows_in = xbuf[pl.ds(begin, 4)].reshape(256, D)
            at = pl.multiple_of(n * 256, 256)
            gate = jnp.dot(rows_in, gu[:, pl.ds(at, 256)], preferred_element_type=F32)
            up = jnp.dot(rows_in, gu[:, pl.ds(FF + at, 256)], preferred_element_type=F32)
            inner[:, pl.ds(at, 256)] = (gate / (1.0 + jnp.exp(-gate)) * up).astype(BF16)
            return carry

        lax.fori_loop(0, FF // 256, hidden, 0)

        def outer(n, carry):
            out = jnp.dot(inner[...], dn[n], preferred_element_type=F32)
            at = pl.multiple_of(n * DN_COLS, DN_COLS)
            ybuf[pl.ds(begin, 4), :, :, pl.ds(at, DN_COLS)] = out.astype(BF16).reshape(4, NX, 16, DN_COLS)
            return carry

        lax.fori_loop(0, NDP, outer, 0, unroll=2)
        for pair in range(3, -1, -1):
            for step in (2, 1, 3):
                target = (x + step) % NX
                remote(
                    ybuf.at[begin + pair, target],
                    ret.at[begin + pair, x],
                    sent.at[YX],
                    yx_recv.at[begin + pair],
                    xpeer(step),
                ).start()
            ret[begin + pair, x] = ybuf[begin + pair, x]
        return carry

    lax.fori_loop(0, 2, chunk_step, 0)

    def up_copy(t, half):
        return remote(up_out.at[t, half], up_in.at[t, half], sent.at[UP], up_recv.at[2 * t + half], above)

    def dn_copy(t, half):
        return remote(dn_out.at[t, half], dn_in.at[t, half], sent.at[DOWN], dn_recv.at[2 * t + half], below)

    def keep(pair):
        arrived(ret.at[pair, pl.ds(0, 3)], yx_recv.at[pair])
        both = jnp.dot(cmat[pair], ret[pair].reshape(64, D), preferred_element_type=F32)
        part[pair] = both.reshape(2, 2, 16, D)

    def reduce_step(t, carry):
        @pl.when(t == 0)
        def _():
            keep(7)

        for half in range(2):
            total = part[7 - t, (8 - t) // 8, half]
            up_out[t, half] = total.astype(BF16)

            @pl.when(t > 0)
            def _():
                arrived(up_in.at[t - 1, half], up_recv.at[2 * (t - 1) + half])
                up_out[t, half] = (up_in[t - 1, half].astype(F32) + total).astype(BF16)

            up_copy(t, half).start()

        @pl.when(t < 7)
        def _():
            keep(6 - t)
            for half in range(2):
                total = part[6 - t, 1, half]
                dn_out[t, half] = total.astype(BF16)

                @pl.when(t > 0)
                def _():
                    arrived(dn_in.at[t - 1, half], dn_recv.at[2 * (t - 1) + half])
                    dn_out[t, half] = (dn_in[t - 1, half].astype(F32) + total).astype(BF16)

                dn_copy(t, half).start()

        return carry

    lax.fori_loop(0, 8, reduce_step, 0)
    for half in range(2):
        rows = slice(half * 16, half * 16 + 16)
        total = held[rows].astype(F32) + part[7, 0, half]
        arrived(dn_in.at[6, half], dn_recv.at[12 + half])
        total += dn_in[6, half].astype(F32)
        arrived(up_in.at[7, half], up_recv.at[14 + half])
        final = (total + up_in[7, half].astype(F32)).astype(BF16)
        stream_ref[rows] = final
        wide = final.astype(F32)
        scale = lax.rsqrt(jnp.mean(wide * wide, axis=-1, keepdims=True) + 1e-06)
        normed_ref[rows] = (wide * scale * gain_final_ref[...]).astype(BF16)

    left_all(W, wbuf.at[pl.ds(0, 15)])
    left_all(A, abuf.at[pl.ds(0, 3)])
    left_all(RS, rbuf.at[pl.ds(0, 7)])
    left_all(SX, sums_out)
    left_all(GU, gu.at[pl.ds(0, 7 * GU_ROWS)])
    left_all(DN, dn.at[pl.ds(0, 7)])
    left_all(NZS, zbuf.at[pl.ds(0, 15)])
    left_all(CX, cbuf.at[pl.ds(0, 6)])
    left_all(YX, ybuf.at[pl.ds(0, 6)])
    left_all(UP, up_out)
    left_all(DOWN, dn_out)


def block(*args):
    vmem = pl.BlockSpec(memory_space=pltpu.VMEM)
    hbm = pl.BlockSpec(memory_space=pl.ANY)
    dma = pltpu.SemaphoreType.DMA
    counts = (5, 11, 16, 6, 2, 1, 6, 3, 2, 32, 8, 8, 16, 14)
    return pl.pallas_call(
        kernel,
        out_shape=[jax.ShapeDtypeStruct((ROWS, D), BF16)] * 2,
        in_specs=[hbm] * 2 + [vmem] * 5 + [hbm] * 2 + [vmem],
        out_specs=[vmem] * 2,
        scratch_shapes=[
            pltpu.VMEM((NX, NDP * ROWS, FB), BF16),
            pltpu.VMEM((ROWS, D), BF16),
            pltpu.VMEM((NZ, ROWS, FB), BF16),
            pltpu.VMEM((NDP, NX, ROWS, FB), BF16),
            pltpu.VMEM((NDP, NX, ROWS, FB), BF16),
            pltpu.VMEM((3, ROWS, FB), BF16),
            pltpu.VMEM((NX, ROWS, FB), BF16),
            pltpu.VMEM((NX, ROWS, FB), F32),
            pltpu.VMEM((ROWS, D), BF16),
            pltpu.VMEM((NZ, 2, 16, D + 128), BF16),
            pltpu.VMEM((PAIRS, NX, 16, D), BF16),
            pltpu.VMEM((PAIRS, NX, 16, D), BF16),
            pltpu.VMEM((PAIRS, 64, 64), BF16),
            pltpu.VMEM((256, FF), BF16),
            pltpu.VMEM((PAIRS, NX, 16, D), BF16),
            pltpu.VMEM((PAIRS, NX, 16, D), BF16),
            pltpu.VMEM((PAIRS, 2, 2, 16, D), F32),
            pltpu.VMEM((8, 2, 16, D), BF16),
            pltpu.VMEM((8, 2, 16, D), BF16),
            pltpu.VMEM((7, 2, 16, D), BF16),
            pltpu.VMEM((7, 2, 16, D), BF16),
            pltpu.VMEM((D, 2 * FF), BF16),
            pltpu.VMEM((NDP, FF, DN_COLS), BF16),
        ]
        + [dma((count,)) for count in counts],
        compiler_params=pltpu.CompilerParams(
            collective_id=0, has_side_effects=True, vmem_limit_bytes=56 << 20
        ),
    )(*args)


def body(
    attn,
    resid,
    w_out,
    gain_post,
    route_ids,
    route_logits,
    live_count,
    w_gate_up,
    w_down,
    gain_final,
):
    stream_out, normed_out = block(
        attn[0],
        resid[0],
        w_out,
        gain_post[None],
        route_ids[0],
        route_logits[0],
        live_count,
        w_gate_up[0],
        w_down[0],
        gain_final[None],
    )
    return (stream_out[None], normed_out[None])


def solution(mesh):
    placed = (
        P("expert", None, "dp"),
        P("expert", "dp", None),
        P("dp", "expert"),
        P(),
        P("expert", "dp", None),
        P("expert", "dp", None),
        P("expert", "dp"),
        P("expert", "dp", None),
        P("expert", None, "dp"),
        P(),
    )
    return jax.shard_map(
        body,
        mesh=mesh,
        in_specs=placed,
        out_specs=(P("expert", "dp", None), P("expert", "dp", None)),
        check_vma=False,
    )
```

time: 446 us -> 143 us (0.32)
  the two profiles are of different devices: /device:TPU:62 before, /device:TPU:4 now
where the time goes in v3:
time: 143 us
  Pallas kernels  136 us (95%)
  local copies, waits for them, and re-layouts  5.75 us (4%)
    pallas_call x1, Pallas kernels, block(): pl.pallas_call(kernel, out_shape=[jax.ShapeDtypeStruct((ROWS, D), BF16)]...  136 us
    unnamed x9, local copies, waits for them, and re-layouts  5.75 us

profile of v3, /device:TPU:4, one launch (start us, length us, event | category | flops | bytes accessed | tf_op | source)
XLA Modules:
  0.0 142.9 jit_solution(1975542992264227881)
XLA Ops:
  0.6 0.0 copy-start.1
  1.3 1.4 copy.12
  2.7 1.4 copy.13
  4.0 0.0 copy-done.1
  4.0 0.8 copy.14.w_ref
  4.8 135.9 %shard_map.113 = (bf16[32,2048]{1,0:T(8,128)(2,1)}, bf16[32,2048]{1,0:T(8,128)(2,1)}) custom-call(bf16[256,512]{1,0:T(8,128)(2,1)} %bitcast.12, bf16[32,2048]{1,0:T(8,128)(2,1)} %bitcast.13, bf16[512,32]{1,0:T(8,128)(2,1)} %copy.14.w_ref, f32[1,2048]{1,0:T(1,128)} %bitcast.18, s32[32,8]{1,0:T(8,128)} %bitcast.16, f32[32,8]{1,0:T(8,128)} %bitcast.17, ...), custom_call_target="tpu_custom_call" | custom-call | tf_op jit(solution)/shard_map/pallas_call | solution.py:480
  140.7 0.0 copy-start
  140.7 1.6 %copy.18 = bf16[1,32,2048]{2,1,0:T(8,128)(2,1)} copy(bf16[1,32,2048]{2,1,0:T(8,128)(2,1)} %bitcast.15) | data formatting | bytes 262144
  142.3 0.0 copy-done
  142.3 0.7 copy.19
Async XLA Ops:
  0.6 3.4 %copy-start.1 = (bf16[512,32]{0,1:T(8,128)(2,1)S(1)}, bf16[512,32]{0,1:T(8,128)(2,1)}, u32[]{:S(2)}) copy-start(bf16[512,32]{0,1:T(8,128)(2,1)} %param.12) | copy-start | bytes 98308
  140.7 1.6 %copy-start = (bf16[32,2048]{1,0:T(8,128)(2,1)S(1)}, bf16[32,2048]{1,0:T(8,128)(2,1)}, u32[]{:S(2)}) copy-start(bf16[32,2048]{1,0:T(8,128)(2,1)} %get-tuple-element.5) | copy-start | bytes 393220

commit v4 on v3

--- a/solution.py
+++ b/solution.py
@@ -43,6 +43,8 @@
     resid,
     wbuf,
     pbuf,
+    qbuf,
+    sbuf,
     rbuf,
     sums_out,
     sums_in,
@@ -56,16 +58,15 @@
     ybuf,
     ret,
     part,
-    up_out,
-    up_in,
-    dn_out,
-    dn_in,
+    rs_out,
+    rs_in,
     gu,
     dn,
     own_sem,
     sent,
     w_recv,
     a_recv,
+    pair_recv,
     rs_recv,
     sx_recv,
     near_recv,
@@ -74,24 +75,27 @@
     nz_recv,
     cx_recv,
     yx_recv,
-    up_recv,
-    dn_recv,
+    ring_recv,
 ):
     dp = lax.axis_index("dp")
     expert = lax.axis_index("expert")
     x, z = expert // NZ, expert % NZ
     y, core = dp // NC, dp % NC
-    zpeer = {step: (dp, x * NZ + (z + NZ + step) % NZ) for step in (-2, -1, 1, 2)}
+    zpeer = {step: (dp, x * NZ + (z + NZ + step) % NZ) for step in (-6, -3, -2, -1, 1, 2, 3, 6)}
     above, below = zpeer[1], zpeer[-1]
 
     def xpeer(step):
         return (dp, (x + step) % NX * NZ + z)
 
     right, left = xpeer(1), xpeer(3)
-    y_up, y_down = ((y + 1) % NY * NC + core, expert), ((y + NY - 1) % NY * NC + core, expert)
+
+    def ypeer(step):
+        return ((y + step) % NY * NC + core, expert)
+
+    y_up, y_down = ypeer(1), ypeer(3)
     sibling = (y * NC + 1 - core, expert)
 
-    W, A, RS, SX, GU, DN, NZS, CX, YX, UP, DOWN = range(11)
+    W, A, PAIR, RS, SX, GU, DN, NZS, CX, YX, UP = range(11)
 
     def left_all(kind, ref):
         remote(ref, ref, sent.at[kind], rs_recv.at[0], right).wait_send()
@@ -106,12 +110,10 @@
     resid_in = local(resid_ref, resid, 4)
     attn_in.start()
     resid_in.start()
-    same = lax.broadcasted_iota(jnp.int32, (ROWS, ROWS), 0) == lax.broadcasted_iota(jnp.int32, (ROWS, ROWS), 1)
-    eye = jnp.where(same, 1.0, 0.0).astype(BF16)
-    wbuf[z] = lax.dot_general(eye, w_ref[...], NT, preferred_element_type=F32).astype(BF16)
+    wbuf[z] = w_ref[...]
 
     peers = list(zpeer.values()) + [xpeer(step) for step in range(1, NX)]
-    peers += [((dp + step) % NDP, expert) for step in range(1, NDP)]
+    peers += [ypeer(step) for step in range(1, NY)] + [sibling]
     barrier = pltpu.get_barrier_semaphore()
     for peer in peers:
         pl.semaphore_signal(barrier, inc=1, device_id=peer, device_id_type=MESH)
@@ -120,10 +122,11 @@
     def z_at(side, h):
         return (z + (h if side == 0 else NZ - h)) % NZ
 
+    jumps = {6: 6, 3: 3, 1: 1, 8: 2, 7: 1, 5: 2, 4: 1, 2: 1}
+
     def w_copy(side, h):
-        ref = wbuf.at[z_at(side, max(h - 2, 0))]
-        step = (1 if side else -1) * min(h, 2)
-        return remote(ref, ref, sent.at[W], w_recv.at[side * 8 + h - 1], zpeer[step])
+        ref = wbuf.at[z_at(side, h - jumps[h])]
+        return remote(ref, ref, sent.at[W], w_recv.at[side * 8 + h - 1], zpeer[jumps[h] if side else -jumps[h]])
 
     def half_rows(half):
         return pl.ds(half * 128, 128)
@@ -139,7 +142,7 @@
     def a_arrived(way, half):
         arrived(abuf.at[(x + (3, 1, 2)[way]) % NX, half_rows(half)], a_recv.at[way * 2 + half])
 
-    for h in (1, 2):
+    for h in (6, 3, 1):
         w_copy(1, h).start()
         w_copy(0, h).start()
     for half in range(2):
@@ -191,14 +194,14 @@
         own_copy(number).start()
 
     logits = logits_ref[...]
-    raised = jnp.exp(logits - jnp.max(logits, axis=1, keepdims=True))
-    probs = (raised / jnp.sum(raised, axis=1, keepdims=True)).astype(BF16)
+    raised = jnp.exp(logits - jnp.max(logits, axis=0, keepdims=True))
+    probs = (raised / jnp.sum(raised, axis=0, keepdims=True)).astype(BF16)
     fold = jnp.where(
         lax.broadcasted_iota(jnp.int32, (ROWS, 128), 1) % ROWS == lax.broadcasted_iota(jnp.int32, (ROWS, 128), 0), 1.0, 0.0
     ).astype(BF16)
     ids = ids_ref[...].astype(F32).astype(BF16)
-    ids_t = lax.dot_general(ids, fold, (((0,), (0,)), ((), ())), preferred_element_type=F32)
-    probs_t = lax.dot_general(probs, fold, (((0,), (0,)), ((), ())), preferred_element_type=F32)
+    ids_t = jnp.dot(ids, fold, preferred_element_type=F32)
+    probs_t = jnp.dot(probs, fold, preferred_element_type=F32)
     lane = lax.broadcasted_iota(jnp.int32, (NZ, 128), 1)
     named = (lane // ROWS * NZ + lax.broadcasted_iota(jnp.int32, (NZ, 128), 0)).astype(F32)
     chosen = jnp.zeros((NZ, 128), F32)
@@ -212,20 +215,24 @@
     col_l = lax.broadcasted_iota(jnp.int32, (128, 128), 1)
     before = jnp.where((row_l // ROWS == col_l // ROWS) & (row_l < col_l), 1.0, 0.0).astype(BF16)
     rank = jnp.dot(chosen.astype(BF16), before, preferred_element_type=F32)
-    zbuf[z, 0, :, D:] = jnp.where(chosen > 0.5, rank, -1.0).astype(BF16)
-    zbuf[z, 1, :, D:] = weight.astype(BF16)
-
-    for h in range(1, 9):
+    zbuf[z, 0:NZ, D:] = jnp.where(chosen > 0.5, rank, -1.0).astype(BF16)
+    zbuf[z, NZ:, D:] = weight.astype(BF16)
+
+    for h, onwards in ((1, (2,)), (3, (5, 4)), (6, (8, 7))):
         for side in (1, 0):
-            if h <= 7 + side:
-                arrived(wbuf.at[z_at(side, h)], w_recv.at[side * 8 + h - 1])
-                if h + 2 <= 7 + side:
-                    w_copy(side, h + 2).start()
-        if h == 2:
+            arrived(wbuf.at[z_at(side, h)], w_recv.at[side * 8 + h - 1])
+            for far in onwards:
+                if far <= 7 + side:
+                    w_copy(side, far).start()
+        if h == 3:
             a_arrived(0, 0)
             a_copy(2, 0).start()
             a_arrived(1, 1)
             a_copy(2, 1).start()
+    for h in (2, 4, 5, 7, 8):
+        for side in (1, 0):
+            if h <= 7 + side:
+                arrived(wbuf.at[z_at(side, h)], w_recv.at[side * 8 + h - 1])
     attn_in.wait()
     resid_in.wait()
     for way, half in ((0, 1), (1, 0), (2, 0), (2, 1)):
@@ -235,29 +242,33 @@
         got = lax.dot_general(
             abuf[(x + 3 - order) % NX], wbuf[...].reshape(FB, FB), NT, preferred_element_type=F32
         )
-        pbuf[:, order] = got.astype(BF16).reshape(NDP, ROWS, FB)
-
-        @pl.when(order % 2 == 1)
-        def _():
-            pair = pl.ds(order - 1, 2)
-            for step in (4, 3, 5, 2, 6, 1, 7):
-                target = (dp + step) % NDP
-                remote(
-                    pbuf.at[target, pair], rbuf.at[dp, pair], sent.at[RS], rs_recv.at[order // 2], (target, expert)
-                ).start()
-
+        blocks = got.astype(BF16).reshape(NY, NC, ROWS, FB)
+        for half in range(NC):
+            pbuf[half, :, order] = blocks[:, half]
+        remote(
+            pbuf.at[1 - core, :, order], qbuf.at[:, order], sent.at[PAIR], pair_recv.at[order], sibling
+        ).start()
         return carry
 
     lax.fori_loop(0, NX, product, 0)
 
+    def exchange(order, carry):
+        arrived(qbuf.at[:, order], pair_recv.at[order])
+        sbuf[:, order] = (pbuf[core, :, order].astype(F32) + qbuf[:, order].astype(F32)).astype(BF16)
+        for step in (2, 1, 3):
+            target = (y + step) % NY
+            remote(
+                sbuf.at[target, order], rbuf.at[y, order], sent.at[RS], rs_recv.at[order], ypeer(step)
+            ).start()
+        return carry
+
+    lax.fori_loop(0, NX, exchange, 0)
+
     def sum_up(order, carry):
-        @pl.when(order % 2 == 0)
-        def _():
-            arrived(rbuf.at[pl.ds(0, 7), pl.ds(0, 2)], rs_recv.at[order // 2])
-
-        total = pbuf[dp, order].astype(F32)
-        for step in range(1, NDP):
-            total += rbuf[(dp + step) % NDP, order].astype(F32)
+        arrived(rbuf.at[pl.ds(0, 3), order], rs_recv.at[order])
+        total = pbuf[core, y, order].astype(F32) + qbuf[y, order].astype(F32)
+        for step in range(1, NY):
+            total += rbuf[(y + step) % NY, order].astype(F32)
 
         @pl.when(order < 3)
         def _():
@@ -298,15 +309,18 @@
         square += jnp.sum(wide * wide, axis=-1, keepdims=True)
     scale = lax.rsqrt(square / D + 1e-06)
     normed = (held[...].astype(F32) * scale * gain_post_ref[...]).astype(BF16)
-    zbuf[z, :, :, 0:D] = normed.reshape(2, 16, D)
-
-    def nz_copy(side, h, half):
-        ref = zbuf.at[z_at(side, h), half]
-        return remote(ref, ref, sent.at[NZS], nz_recv.at[(side * 8 + h) * 2 + half], above if side else below)
-
-    for half in range(2):
-        nz_copy(1, 0, half).start()
-        nz_copy(0, 0, half).start()
+    zbuf[z, :, 0:D] = normed
+
+    def row_chunk(side, h, c):
+        return zbuf.at[z_at(side, h), :, pl.ds(c * FB, FB if c < 3 else FB + 128)]
+
+    def nz_copy(side, h, c):
+        ref = row_chunk(side, h, c)
+        return remote(ref, ref, sent.at[NZS], nz_recv.at[(side * 8 + h) * 4 + c], above if side else below)
+
+    for c in range(4):
+        nz_copy(1, 0, c).start()
+        nz_copy(0, 0, c).start()
 
     slot_i = lax.broadcasted_iota(jnp.int32, (64, 128), 0)
     slot_l = lax.broadcasted_iota(jnp.int32, (64, 128), 1)
@@ -316,7 +330,7 @@
     here = lax.broadcasted_iota(jnp.int32, (NZ, 128), 0) == z
 
     def table_row(source, half):
-        table = zbuf[source, half, :, D:].astype(F32)
+        table = zbuf[source, half * NZ : (half + 1) * NZ, D:].astype(F32)
         return jnp.sum(jnp.where(here, table, 0.0), axis=0, keepdims=True)
 
     def compact(h):
@@ -328,7 +342,7 @@
             scaled = jnp.where(hit, table_row(source, 1), 0.0).astype(BF16)
             spread = lax.dot_general(fold, scaled, NT, preferred_element_type=F32)
             cmat[h - 1, side * ROWS : (side + 1) * ROWS] = spread.astype(BF16)
-            total += jnp.dot(choose, zbuf[source, :, :, 0:D].reshape(ROWS, D), preferred_element_type=F32)
+            total += jnp.dot(choose, zbuf[source, :, 0:D], preferred_element_type=F32)
         cbuf[h - 1] = total.astype(BF16).reshape(NX, 16, D)
         for step in (2, 1, 3):
             target = (x + step) % NX
@@ -338,16 +352,17 @@
         xbuf[h - 1, x] = cbuf[h - 1, x]
 
     def ring_step(h, carry):
-        for half in range(2):
+        for c in range(4):
             for side in (1, 0):
-
-                @pl.when(h <= 7 + side)
+                last = 8 if (c < 2) == (side == 1) else 7
+
+                @pl.when(h <= last)
                 def _():
-                    arrived(zbuf.at[z_at(side, h), half], nz_recv.at[(side * 8 + h - 1) * 2 + half])
-
-                @pl.when(h < 7 + side)
+                    arrived(row_chunk(side, h, c), nz_recv.at[(side * 8 + h - 1) * 4 + c])
+
+                @pl.when(h < last)
                 def _():
-                    nz_copy(side, h, half).start()
+                    nz_copy(side, h, c).start()
 
 
         @pl.when(h == 7)
@@ -403,80 +418,89 @@
 
     lax.fori_loop(0, 2, chunk_step, 0)
 
-    def up_copy(t, half):
-        return remote(up_out.at[t, half], up_in.at[t, half], sent.at[UP], up_recv.at[2 * t + half], above)
-
-    def dn_copy(t, half):
-        return remote(dn_out.at[t, half], dn_in.at[t, half], sent.at[DOWN], dn_recv.at[2 * t + half], below)
-
     def keep(pair):
         arrived(ret.at[pair, pl.ds(0, 3)], yx_recv.at[pair])
         both = jnp.dot(cmat[pair], ret[pair].reshape(64, D), preferred_element_type=F32)
-        part[pair] = both.reshape(2, 2, 16, D)
+        part[pair] = both.reshape(2, ROWS, D)
+
+    def sum_copy(way, t, c):
+        return remote(
+            rs_out.at[way, t, c], rs_in.at[way, t, c], sent.at[UP + way], ring_recv.at[(way * 8 + t) * 4 + c],
+            (above, below)[way],
+        )
+
+    def sum_arrived(way, t, c):
+        arrived(rs_in.at[way, t, c], ring_recv.at[(way * 8 + t) * 4 + c])
+
+    def cols(c):
+        return slice(c * FB, (c + 1) * FB)
+
+    keep(7)
+    for c in (0, 1):
+        for way in range(2):
+            rs_out[way, 0, 2 * way + c] = part[7, 1, :, cols(2 * way + c)].astype(BF16)
+            sum_copy(way, 0, 2 * way + c).start()
+    keep(6)
+    for c in (0, 1):
+        for way in range(2):
+            rs_out[way, 1, 2 - 2 * way + c] = part[6, way, :, cols(2 - 2 * way + c)].astype(BF16)
+            sum_copy(way, 1, 2 - 2 * way + c).start()
 
     def reduce_step(t, carry):
-        @pl.when(t == 0)
+        def forward(way, c):
+            sum_arrived(way, t - 1, c)
+            rs_out[way, t, c] = (rs_in[way, t - 1, c].astype(F32) + part[7 - t, way, :, cols(c)]).astype(BF16)
+            sum_copy(way, t, c).start()
+
+        for c in (0, 1):
+            for way in range(2):
+                forward(way, 2 * way + c)
+
+        @pl.when(t > 1)
         def _():
-            keep(7)
-
-        for half in range(2):
-            total = part[7 - t, (8 - t) // 8, half]
-            up_out[t, half] = total.astype(BF16)
-
-            @pl.when(t > 0)
-            def _():
-                arrived(up_in.at[t - 1, half], up_recv.at[2 * (t - 1) + half])
-                up_out[t, half] = (up_in[t - 1, half].astype(F32) + total).astype(BF16)
-
-            up_copy(t, half).start()
+            for c in (0, 1):
+                for way in range(2):
+                    forward(way, 2 - 2 * way + c)
 
         @pl.when(t < 7)
         def _():
             keep(6 - t)
-            for half in range(2):
-                total = part[6 - t, 1, half]
-                dn_out[t, half] = total.astype(BF16)
-
-                @pl.when(t > 0)
-                def _():
-                    arrived(dn_in.at[t - 1, half], dn_recv.at[2 * (t - 1) + half])
-                    dn_out[t, half] = (dn_in[t - 1, half].astype(F32) + total).astype(BF16)
-
-                dn_copy(t, half).start()
 
         return carry
 
-    lax.fori_loop(0, 8, reduce_step, 0)
-    for half in range(2):
-        rows = slice(half * 16, half * 16 + 16)
-        total = held[rows].astype(F32) + part[7, 0, half]
-        arrived(dn_in.at[6, half], dn_recv.at[12 + half])
-        total += dn_in[6, half].astype(F32)
-        arrived(up_in.at[7, half], up_recv.at[14 + half])
-        final = (total + up_in[7, half].astype(F32)).astype(BF16)
-        stream_ref[rows] = final
+    lax.fori_loop(1, 8, reduce_step, 0)
+    square = jnp.zeros((ROWS, 1), F32)
+    for c in (0, 2, 1, 3):
+        total = held[:, cols(c)].astype(F32) + part[7, 0, :, cols(c)]
+        for way in range(2):
+            sum_arrived(way, 7, c)
+            total += rs_in[way, 7, c].astype(F32)
+        final = total.astype(BF16)
+        stream_ref[:, cols(c)] = final
         wide = final.astype(F32)
-        scale = lax.rsqrt(jnp.mean(wide * wide, axis=-1, keepdims=True) + 1e-06)
-        normed_ref[rows] = (wide * scale * gain_final_ref[...]).astype(BF16)
+        square += jnp.sum(wide * wide, axis=-1, keepdims=True)
+    scale = lax.rsqrt(square / D + 1e-06)
+    normed_ref[...] = (stream_ref[...].astype(F32) * scale * gain_final_ref[...]).astype(BF16)
 
     left_all(W, wbuf.at[pl.ds(0, 15)])
     left_all(A, abuf.at[pl.ds(0, 3)])
-    left_all(RS, rbuf.at[pl.ds(0, 7)])
+    left_all(PAIR, qbuf)
+    left_all(RS, rbuf.at[pl.ds(0, 3)])
     left_all(SX, sums_out)
     left_all(GU, gu.at[pl.ds(0, 7 * GU_ROWS)])
     left_all(DN, dn.at[pl.ds(0, 7)])
     left_all(NZS, zbuf.at[pl.ds(0, 15)])
     left_all(CX, cbuf.at[pl.ds(0, 6)])
     left_all(YX, ybuf.at[pl.ds(0, 6)])
-    left_all(UP, up_out)
-    left_all(DOWN, dn_out)
+    for way in range(2):
+        left_all(UP + way, xbuf.at[pl.ds(0, 5), pl.ds(0, 3)])
 
 
 def block(*args):
     vmem = pl.BlockSpec(memory_space=pltpu.VMEM)
     hbm = pl.BlockSpec(memory_space=pl.ANY)
     dma = pltpu.SemaphoreType.DMA
-    counts = (5, 11, 16, 6, 2, 1, 6, 3, 2, 32, 8, 8, 16, 14)
+    counts = (5, 12, 16, 6, 4, 4, 1, 6, 3, 2, 64, 8, 8, 64)
     return pl.pallas_call(
         kernel,
         out_shape=[jax.ShapeDtypeStruct((ROWS, D), BF16)] * 2,
@@ -486,24 +510,24 @@
             pltpu.VMEM((NX, NDP * ROWS, FB), BF16),
             pltpu.VMEM((ROWS, D), BF16),
             pltpu.VMEM((NZ, ROWS, FB), BF16),
-            pltpu.VMEM((NDP, NX, ROWS, FB), BF16),
-            pltpu.VMEM((NDP, NX, ROWS, FB), BF16),
+            pltpu.VMEM((NC, NY, NX, ROWS, FB), BF16),
+            pltpu.VMEM((NY, NX, ROWS, FB), BF16),
+            pltpu.VMEM((NY, NX, ROWS, FB), BF16),
+            pltpu.VMEM((NY, NX, ROWS, FB), BF16),
             pltpu.VMEM((3, ROWS, FB), BF16),
             pltpu.VMEM((NX, ROWS, FB), BF16),
             pltpu.VMEM((NX, ROWS, FB), F32),
             pltpu.VMEM((ROWS, D), BF16),
-            pltpu.VMEM((NZ, 2, 16, D + 128), BF16),
+            pltpu.VMEM((NZ, ROWS, D + 128), BF16),
             pltpu.VMEM((PAIRS, NX, 16, D), BF16),
             pltpu.VMEM((PAIRS, NX, 16, D), BF16),
             pltpu.VMEM((PAIRS, 64, 64), BF16),
             pltpu.VMEM((256, FF), BF16),
             pltpu.VMEM((PAIRS, NX, 16, D), BF16),
             pltpu.VMEM((PAIRS, NX, 16, D), BF16),
-            pltpu.VMEM((PAIRS, 2, 2, 16, D), F32),
-            pltpu.VMEM((8, 2, 16, D), BF16),
-            pltpu.VMEM((8, 2, 16, D), BF16),
-            pltpu.VMEM((7, 2, 16, D), BF16),
-            pltpu.VMEM((7, 2, 16, D), BF16),
+            pltpu.VMEM((PAIRS, 2, ROWS, D), F32),
+            pltpu.VMEM((2, 8, 4, ROWS, FB), BF16),
+            pltpu.VMEM((2, 8, 4, ROWS, FB), BF16),
             pltpu.VMEM((D, 2 * FF), BF16),
             pltpu.VMEM((NDP, FF, DN_COLS), BF16),
         ]
@@ -529,10 +553,10 @@
     stream_out, normed_out = block(
         attn[0],
         resid[0],
-        w_out,
+        w_out.T,
         gain_post[None],
-        route_ids[0],
-        route_logits[0],
+        route_ids[0].T,
+        route_logits[0].T,
         live_count,
         w_gate_up[0],
         w_down[0],

time: 143 us -> 132 us (0.923)
  the two profiles are of different devices: /device:TPU:4 before, /device:TPU:32 now
where the time goes in v4:
time: 132 us
  Pallas kernels  128 us (97%)
  local copies, waits for them, and re-layouts  2.26 us (2%)
    pallas_call x1, Pallas kernels, block(): pl.pallas_call(kernel, out_shape=[jax.ShapeDtypeStruct((ROWS, D), BF16)]...  128 us

profile of v4, /device:TPU:32, one launch (start us, length us, event | category | flops | bytes accessed | tf_op | source)
XLA Modules:
  0.0 131.9 jit_solution(8401917261386592234)
XLA Ops:
  1.3 128.3 %shard_map.113 = (bf16[32,2048]{1,0:T(8,128)(2,1)}, bf16[32,2048]{1,0:T(8,128)(2,1)}) custom-call(bf16[256,512]{1,0:T(8,128)(2,1)} %bitcast.17, bf16[32,2048]{1,0:T(8,128)(2,1)} %bitcast.18, bf16[32,512]{1,0:T(8,128)(2,1)} %bitcast.21, f32[1,2048]{1,0:T(1,128)} %bitcast.22, s32[8,32]{1,0:T(8,128)} %bitcast.24, f32[8,32]{1,0:T(8,128)} %bitcast.25, ...), custom_call_target="tpu_custom_call" | custom-call | tf_op jit(solution)/shard_map/pallas_call | solution.py:504
  129.6 0.0 copy-start
  129.6 1.6 %copy.15 = bf16[1,32,2048]{2,1,0:T(8,128)(2,1)} copy(bf16[1,32,2048]{2,1,0:T(8,128)(2,1)} %bitcast.20) | data formatting | bytes 262144
  131.2 0.0 copy-done
  131.2 0.7 copy.16
Async XLA Ops:
  129.6 1.6 %copy-start = (bf16[32,2048]{1,0:T(8,128)(2,1)S(1)}, bf16[32,2048]{1,0:T(8,128)(2,1)}, u32[]{:S(2)}) copy-start(bf16[32,2048]{1,0:T(8,128)(2,1)} %get-tuple-element.5) | copy-start | bytes 393220

commit v5 on v4

--- a/solution.py
+++ b/solution.py
@@ -10,6 +10,8 @@
 ROWS, D, FB, FF, TOP, CAP = 32, 2048, 512, 768, 8, 8
 GU_ROWS, DN_COLS, CUT = D // NDP, D // NDP, 192
 PAIRS = NZ // 2
+CHUNKS = 4
+WIDE, HALF = D // CHUNKS, CHUNKS // 2
 MESH = pl.DeviceIdType.MESH
 F32, BF16 = jnp.float32, jnp.bfloat16
 NT = (((1,), (1,)), ((), ()))
@@ -50,6 +52,8 @@
     sums_in,
     sums,
     held,
+    table_out,
+    table_in,
     zbuf,
     cbuf,
     xbuf,
@@ -66,6 +70,7 @@
     sent,
     w_recv,
     a_recv,
+    table_recv,
     pair_recv,
     rs_recv,
     sx_recv,
@@ -81,7 +86,7 @@
     expert = lax.axis_index("expert")
     x, z = expert // NZ, expert % NZ
     y, core = dp // NC, dp % NC
-    zpeer = {step: (dp, x * NZ + (z + NZ + step) % NZ) for step in (-6, -3, -2, -1, 1, 2, 3, 6)}
+    zpeer = {step: (dp, x * NZ + (z + NZ + step) % NZ) for step in range(-7, 9) if step}
     above, below = zpeer[1], zpeer[-1]
 
     def xpeer(step):
@@ -95,7 +100,7 @@
     y_up, y_down = ypeer(1), ypeer(3)
     sibling = (y * NC + 1 - core, expert)
 
-    W, A, PAIR, RS, SX, GU, DN, NZS, CX, YX, UP = range(11)
+    W, A, TABLE, PAIR, RS, SX, GU, DN, NZS, CX, YX, UP = range(12)
 
     def left_all(kind, ref):
         remote(ref, ref, sent.at[kind], rs_recv.at[0], right).wait_send()
@@ -215,8 +220,14 @@
     col_l = lax.broadcasted_iota(jnp.int32, (128, 128), 1)
     before = jnp.where((row_l // ROWS == col_l // ROWS) & (row_l < col_l), 1.0, 0.0).astype(BF16)
     rank = jnp.dot(chosen.astype(BF16), before, preferred_element_type=F32)
-    zbuf[z, 0:NZ, D:] = jnp.where(chosen > 0.5, rank, -1.0).astype(BF16)
-    zbuf[z, NZ:, D:] = weight.astype(BF16)
+    table_out[...] = jnp.zeros((NZ, 8, 128), F32)
+    table_out[:, 0, :] = jnp.where(chosen > 0.5, rank, -1.0)
+    table_out[:, 1, :] = weight
+    table_in[z] = table_out[z]
+    for step, peer in zpeer.items():
+        remote(
+            table_out.at[(z + NZ + step) % NZ], table_in.at[z], sent.at[TABLE], table_recv.at[0], peer
+        ).start()
 
     for h, onwards in ((1, (2,)), (3, (5, 4)), (6, (8, 7))):
         for side in (1, 0):
@@ -283,6 +294,33 @@
 
     lax.fori_loop(0, NX, sum_up, 0)
 
+    arrived(sums_in.at[pl.ds(0, 3)], sx_recv.at[0])
+    for step in range(1, NX):
+        source = (x + step) % NX
+        sums[source] = sums_in[source].astype(F32)
+
+    square = jnp.zeros((ROWS, 1), F32)
+    for g in range(4):
+        cols = slice(g * FB, (g + 1) * FB)
+        both = (resid[:, cols].astype(F32) + sums[g]).astype(BF16)
+        held[:, cols] = both
+        wide = both.astype(F32)
+        square += jnp.sum(wide * wide, axis=-1, keepdims=True)
+    scale = lax.rsqrt(square / D + 1e-06)
+    normed = (held[...].astype(F32) * scale * gain_post_ref[...]).astype(BF16)
+    zbuf[z] = normed
+
+    def row_chunk(side, h, c):
+        return zbuf.at[z_at(side, h), :, pl.ds(c * WIDE, WIDE)]
+
+    def nz_copy(side, h, c):
+        ref = row_chunk(side, h, c)
+        return remote(ref, ref, sent.at[NZS], nz_recv.at[(side * 8 + h) * CHUNKS + c], above if side else below)
+
+    for c in range(CHUNKS):
+        nz_copy(1, 0, c).start()
+        nz_copy(0, 0, c).start()
+
     for number in range(3):
         near_arrived(0, number)
         near_arrived(1, 2 - number)
@@ -295,54 +333,23 @@
         to_sibling(3, number).start()
         to_sibling(1, number).start()
 
-    arrived(sums_in.at[pl.ds(0, 3)], sx_recv.at[0])
-    for step in range(1, NX):
-        source = (x + step) % NX
-        sums[source] = sums_in[source].astype(F32)
-
-    square = jnp.zeros((ROWS, 1), F32)
-    for g in range(4):
-        cols = slice(g * FB, (g + 1) * FB)
-        both = (resid[:, cols].astype(F32) + sums[g]).astype(BF16)
-        held[:, cols] = both
-        wide = both.astype(F32)
-        square += jnp.sum(wide * wide, axis=-1, keepdims=True)
-    scale = lax.rsqrt(square / D + 1e-06)
-    normed = (held[...].astype(F32) * scale * gain_post_ref[...]).astype(BF16)
-    zbuf[z, :, 0:D] = normed
-
-    def row_chunk(side, h, c):
-        return zbuf.at[z_at(side, h), :, pl.ds(c * FB, FB if c < 3 else FB + 128)]
-
-    def nz_copy(side, h, c):
-        ref = row_chunk(side, h, c)
-        return remote(ref, ref, sent.at[NZS], nz_recv.at[(side * 8 + h) * 4 + c], above if side else below)
-
-    for c in range(4):
-        nz_copy(1, 0, c).start()
-        nz_copy(0, 0, c).start()
-
     slot_i = lax.broadcasted_iota(jnp.int32, (64, 128), 0)
     slot_l = lax.broadcasted_iota(jnp.int32, (64, 128), 1)
     slot_k = (slot_i % CAP).astype(F32)
     slot_x = slot_l // ROWS == slot_i // 16
     slot_side = [slot_x & (slot_i // CAP % 2 == side) for side in range(2)]
-    here = lax.broadcasted_iota(jnp.int32, (NZ, 128), 0) == z
-
-    def table_row(source, half):
-        table = zbuf[source, half * NZ : (half + 1) * NZ, D:].astype(F32)
-        return jnp.sum(jnp.where(here, table, 0.0), axis=0, keepdims=True)
+    arrived(table_in.at[pl.ds(0, NZ - 1)], table_recv.at[0])
 
     def compact(h):
         total = jnp.zeros((64, D), F32)
         for side, source in enumerate((z_at(0, h % PAIRS), z_at(1, h))):
-            hit = slot_side[side] & (table_row(source, 0) == slot_k)
+            hit = slot_side[side] & (table_in[source, 0:1, :] == slot_k)
             picked = jnp.where(hit, 1.0, 0.0).astype(BF16)
             choose = lax.dot_general(picked, fold, NT, preferred_element_type=F32).astype(BF16)
-            scaled = jnp.where(hit, table_row(source, 1), 0.0).astype(BF16)
+            scaled = jnp.where(hit, table_in[source, 1:2, :], 0.0).astype(BF16)
             spread = lax.dot_general(fold, scaled, NT, preferred_element_type=F32)
             cmat[h - 1, side * ROWS : (side + 1) * ROWS] = spread.astype(BF16)
-            total += jnp.dot(choose, zbuf[source, :, 0:D], preferred_element_type=F32)
+            total += jnp.dot(choose, zbuf[source], preferred_element_type=F32)
         cbuf[h - 1] = total.astype(BF16).reshape(NX, 16, D)
         for step in (2, 1, 3):
             target = (x + step) % NX
@@ -352,13 +359,13 @@
         xbuf[h - 1, x] = cbuf[h - 1, x]
 
     def ring_step(h, carry):
-        for c in range(4):
+        for c in range(CHUNKS):
             for side in (1, 0):
-                last = 8 if (c < 2) == (side == 1) else 7
+                last = 8 if (c < HALF) == (side == 1) else 7
 
                 @pl.when(h <= last)
                 def _():
-                    arrived(row_chunk(side, h, c), nz_recv.at[(side * 8 + h - 1) * 4 + c])
+                    arrived(row_chunk(side, h, c), nz_recv.at[(side * 8 + h - 1) * CHUNKS + c])
 
                 @pl.when(h < last)
                 def _():
@@ -381,42 +388,49 @@
     for number in range(3):
         own_copy(number).wait()
 
-    def chunk_step(order, carry):
-        begin = (1 - order) * 4
-        for pair in range(4):
+    def experts(begin, count):
+        rows = count * 64
+        for pair in range(count):
             arrived(xbuf.at[begin + pair, pl.ds(0, 3)], cx_recv.at[begin + pair])
 
         def hidden(n, carry):
-            rows_in = xbuf[pl.ds(begin, 4)].reshape(256, D)
+            rows_in = xbuf[pl.ds(begin, count)].reshape(rows, D)
             at = pl.multiple_of(n * 256, 256)
             gate = jnp.dot(rows_in, gu[:, pl.ds(at, 256)], preferred_element_type=F32)
             up = jnp.dot(rows_in, gu[:, pl.ds(FF + at, 256)], preferred_element_type=F32)
-            inner[:, pl.ds(at, 256)] = (gate / (1.0 + jnp.exp(-gate)) * up).astype(BF16)
+            inner[0:rows, pl.ds(at, 256)] = (gate / (1.0 + jnp.exp(-gate)) * up).astype(BF16)
             return carry
 
         lax.fori_loop(0, FF // 256, hidden, 0)
 
         def outer(n, carry):
-            out = jnp.dot(inner[...], dn[n], preferred_element_type=F32)
+            out = jnp.dot(inner[0:rows], dn[n], preferred_element_type=F32)
             at = pl.multiple_of(n * DN_COLS, DN_COLS)
-            ybuf[pl.ds(begin, 4), :, :, pl.ds(at, DN_COLS)] = out.astype(BF16).reshape(4, NX, 16, DN_COLS)
+            ybuf[pl.ds(begin, count), :, :, pl.ds(at, DN_COLS)] = out.astype(BF16).reshape(count, NX, 16, DN_COLS)
             return carry
 
-        lax.fori_loop(0, NDP, outer, 0, unroll=2)
-        for pair in range(3, -1, -1):
-            for step in (2, 1, 3):
-                target = (x + step) % NX
-                remote(
-                    ybuf.at[begin + pair, target],
-                    ret.at[begin + pair, x],
-                    sent.at[YX],
-                    yx_recv.at[begin + pair],
-                    xpeer(step),
-                ).start()
-            ret[begin + pair, x] = ybuf[begin + pair, x]
+        lax.fori_loop(0, NDP, outer, 0, unroll=4)
+
+    def give_back(pair):
+        for step in (2, 1, 3):
+            target = (x + step) % NX
+            remote(
+                ybuf.at[pair, target], ret.at[pair, x], sent.at[YX], yx_recv.at[pair], xpeer(step)
+            ).start()
+        ret[pair, x] = ybuf[pair, x]
+
+    experts(0, 4)
+
+    def chunk_step(order, carry):
+        begin = 6 - 2 * order
+        experts(begin, 2)
+        give_back(begin + 1)
+        give_back(begin)
         return carry
 
     lax.fori_loop(0, 2, chunk_step, 0)
+    for pair in (3, 2, 1, 0):
+        give_back(pair)
 
     def keep(pair):
         arrived(ret.at[pair, pl.ds(0, 3)], yx_recv.at[pair])
@@ -425,26 +439,26 @@
 
     def sum_copy(way, t, c):
         return remote(
-            rs_out.at[way, t, c], rs_in.at[way, t, c], sent.at[UP + way], ring_recv.at[(way * 8 + t) * 4 + c],
+            rs_out.at[way, t, c], rs_in.at[way, t, c], sent.at[UP + way], ring_recv.at[(way * 8 + t) * CHUNKS + c],
             (above, below)[way],
         )
 
     def sum_arrived(way, t, c):
-        arrived(rs_in.at[way, t, c], ring_recv.at[(way * 8 + t) * 4 + c])
+        arrived(rs_in.at[way, t, c], ring_recv.at[(way * 8 + t) * CHUNKS + c])
 
     def cols(c):
-        return slice(c * FB, (c + 1) * FB)
+        return slice(c * WIDE, (c + 1) * WIDE)
 
     keep(7)
-    for c in (0, 1):
+    for c in range(HALF):
         for way in range(2):
-            rs_out[way, 0, 2 * way + c] = part[7, 1, :, cols(2 * way + c)].astype(BF16)
-            sum_copy(way, 0, 2 * way + c).start()
+            rs_out[way, 0, HALF * way + c] = part[7, 1, :, cols(HALF * way + c)].astype(BF16)
+            sum_copy(way, 0, HALF * way + c).start()
     keep(6)
-    for c in (0, 1):
+    for c in range(HALF):
         for way in range(2):
-            rs_out[way, 1, 2 - 2 * way + c] = part[6, way, :, cols(2 - 2 * way + c)].astype(BF16)
-            sum_copy(way, 1, 2 - 2 * way + c).start()
+            rs_out[way, 1, HALF * (1 - way) + c] = part[6, way, :, cols(HALF * (1 - way) + c)].astype(BF16)
+            sum_copy(way, 1, HALF * (1 - way) + c).start()
 
     def reduce_step(t, carry):
         def forward(way, c):
@@ -452,15 +466,15 @@
             rs_out[way, t, c] = (rs_in[way, t - 1, c].astype(F32) + part[7 - t, way, :, cols(c)]).astype(BF16)
             sum_copy(way, t, c).start()
 
-        for c in (0, 1):
+        for c in range(HALF):
             for way in range(2):
-                forward(way, 2 * way + c)
+                forward(way, HALF * way + c)
 
         @pl.when(t > 1)
         def _():
-            for c in (0, 1):
+            for c in range(HALF):
                 for way in range(2):
-                    forward(way, 2 - 2 * way + c)
+                    forward(way, HALF * (1 - way) + c)
 
         @pl.when(t < 7)
         def _():
@@ -470,7 +484,7 @@
 
     lax.fori_loop(1, 8, reduce_step, 0)
     square = jnp.zeros((ROWS, 1), F32)
-    for c in (0, 2, 1, 3):
+    for c in range(CHUNKS):
         total = held[:, cols(c)].astype(F32) + part[7, 0, :, cols(c)]
         for way in range(2):
             sum_arrived(way, 7, c)
@@ -484,6 +498,7 @@
 
     left_all(W, wbuf.at[pl.ds(0, 15)])
     left_all(A, abuf.at[pl.ds(0, 3)])
+    left_all(TABLE, table_out.at[pl.ds(0, NZ - 1)])
     left_all(PAIR, qbuf)
     left_all(RS, rbuf.at[pl.ds(0, 3)])
     left_all(SX, sums_out)
@@ -500,7 +515,7 @@
     vmem = pl.BlockSpec(memory_space=pltpu.VMEM)
     hbm = pl.BlockSpec(memory_space=pl.ANY)
     dma = pltpu.SemaphoreType.DMA
-    counts = (5, 12, 16, 6, 4, 4, 1, 6, 3, 2, 64, 8, 8, 64)
+    counts = (5, 13, 16, 6, 1, 4, 4, 1, 6, 3, 2, 16 * CHUNKS, 8, 8, 16 * CHUNKS)
     return pl.pallas_call(
         kernel,
         out_shape=[jax.ShapeDtypeStruct((ROWS, D), BF16)] * 2,
@@ -518,7 +533,9 @@
             pltpu.VMEM((NX, ROWS, FB), BF16),
             pltpu.VMEM((NX, ROWS, FB), F32),
             pltpu.VMEM((ROWS, D), BF16),
-            pltpu.VMEM((NZ, ROWS, D + 128), BF16),
+            pltpu.VMEM((NZ, 8, 128), F32),
+            pltpu.VMEM((NZ, 8, 128), F32),
+            pltpu.VMEM((NZ, ROWS, D), BF16),
             pltpu.VMEM((PAIRS, NX, 16, D), BF16),
             pltpu.VMEM((PAIRS, NX, 16, D), BF16),
             pltpu.VMEM((PAIRS, 64, 64), BF16),
@@ -526,8 +543,8 @@
             pltpu.VMEM((PAIRS, NX, 16, D), BF16),
             pltpu.VMEM((PAIRS, NX, 16, D), BF16),
             pltpu.VMEM((PAIRS, 2, ROWS, D), F32),
-            pltpu.VMEM((2, 8, 4, ROWS, FB), BF16),
-            pltpu.VMEM((2, 8, 4, ROWS, FB), BF16),
+            pltpu.VMEM((2, 8, CHUNKS, ROWS, WIDE), BF16),
+            pltpu.VMEM((2, 8, CHUNKS, ROWS, WIDE), BF16),
             pltpu.VMEM((D, 2 * FF), BF16),
             pltpu.VMEM((NDP, FF, DN_COLS), BF16),
         ]

time: 132 us -> 131 us (level)
  no operation moved by 1% of the time
where the time goes in v5:
time: 131 us
  Pallas kernels  128 us (98%)
  local copies, waits for them, and re-layouts  2.26 us (2%)
    pallas_call x1, Pallas kernels, block(): pl.pallas_call(kernel, out_shape=[jax.ShapeDtypeStruct((ROWS, D), BF16)]...  128 us

profile of v5, /device:TPU:32, one launch (start us, length us, event | category | flops | bytes accessed | tf_op | source)
XLA Modules:
  0.0 131.2 jit_solution(17359810883541883135)
XLA Ops:
  1.3 127.7 %shard_map.113 = (bf16[32,2048]{1,0:T(8,128)(2,1)}, bf16[32,2048]{1,0:T(8,128)(2,1)}) custom-call(bf16[256,512]{1,0:T(8,128)(2,1)} %bitcast.17, bf16[32,2048]{1,0:T(8,128)(2,1)} %bitcast.18, bf16[32,512]{1,0:T(8,128)(2,1)} %bitcast.21, f32[1,2048]{1,0:T(1,128)} %bitcast.22, s32[8,32]{1,0:T(8,128)} %bitcast.24, f32[8,32]{1,0:T(8,128)} %bitcast.25, ...), custom_call_target="tpu_custom_call" | custom-call | tf_op jit(solution)/shard_map/pallas_call | solution.py:519
  128.9 0.0 copy-start
  129.0 1.6 %copy.15 = bf16[1,32,2048]{2,1,0:T(8,128)(2,1)} copy(bf16[1,32,2048]{2,1,0:T(8,128)(2,1)} %bitcast.20) | data formatting | bytes 262144
  130.6 0.0 copy-done
  130.6 0.7 copy.16
Async XLA Ops:
  128.9 1.6 %copy-start = (bf16[32,2048]{1,0:T(8,128)(2,1)S(1)}, bf16[32,2048]{1,0:T(8,128)(2,1)}, u32[]{:S(2)}) copy-start(bf16[32,2048]{1,0:T(8,128)(2,1)} %get-tuple-element.5) | copy-start | bytes 393220

commit v6 on v5

--- a/solution.py
+++ b/solution.py
@@ -191,9 +191,9 @@
     def own_copy(number):
         return local(own_piece(number), piece(dp, number), number)
 
-    for number in range(3):
+    for number in range(2):
         to_near(0, number).start()
-        to_near(1, 2 - number).start()
+        to_near(1, 1 - number).start()
     for number in range(3):
         to_sibling(0, number).start()
         own_copy(number).start()
@@ -274,6 +274,8 @@
         return carry
 
     lax.fori_loop(0, NX, exchange, 0)
+    to_near(0, 2).start()
+    to_near(1, 2).start()
 
     def sum_up(order, carry):
         arrived(rbuf.at[pl.ds(0, 3), order], rs_recv.at[order])

time: 131 us -> 127 us (0.969)
  Pallas kernels: 128 us -> 123 us
    pallas_call x1, Pallas kernels: 128 us -> 123 us  [block(): pl.pallas_call(kernel, out_shape=[jax.ShapeDtypeStruct((ROWS, D), BF16)]...]
where the time goes in v6:
time: 127 us
  Pallas kernels  123 us (97%)
  local copies, waits for them, and re-layouts  2.26 us (2%)
  between operations  1.3 us (1%)
    pallas_call x1, Pallas kernels, block(): pl.pallas_call(kernel, out_shape=[jax.ShapeDtypeStruct((ROWS, D), BF16)]...  123 us

profile of v6, /device:TPU:32, one launch (start us, length us, event | category | flops | bytes accessed | tf_op | source)
XLA Modules:
  0.0 126.5 jit_solution(18314344240425178837)
XLA Ops:
  1.3 123.0 %shard_map.113 = (bf16[32,2048]{1,0:T(8,128)(2,1)}, bf16[32,2048]{1,0:T(8,128)(2,1)}) custom-call(bf16[256,512]{1,0:T(8,128)(2,1)} %bitcast.17, bf16[32,2048]{1,0:T(8,128)(2,1)} %bitcast.18, bf16[32,512]{1,0:T(8,128)(2,1)} %bitcast.21, f32[1,2048]{1,0:T(1,128)} %bitcast.22, s32[8,32]{1,0:T(8,128)} %bitcast.24, f32[8,32]{1,0:T(8,128)} %bitcast.25, ...), custom_call_target="tpu_custom_call" | custom-call | tf_op jit(solution)/shard_map/pallas_call | solution.py:521
  124.3 0.0 copy-start
  124.3 1.6 %copy.15 = bf16[1,32,2048]{2,1,0:T(8,128)(2,1)} copy(bf16[1,32,2048]{2,1,0:T(8,128)(2,1)} %bitcast.20) | data formatting | bytes 262144
  125.9 0.0 copy-done
  125.9 0.7 copy.16
Async XLA Ops:
  124.3 1.6 %copy-start = (bf16[32,2048]{1,0:T(8,128)(2,1)S(1)}, bf16[32,2048]{1,0:T(8,128)(2,1)}, u32[]{:S(2)}) copy-start(bf16[32,2048]{1,0:T(8,128)(2,1)} %get-tuple-element.5) | copy-start | bytes 393220
